TPU v7x, 32 devices: a whole 2x2x4 slice. The times are simulated.
32 devices in a mesh: tok: 16 (over z, y, core), tp: 2 (over x).
Axes of the slice: x: 2, y: 2, z: 4, core: 2. Of those that a mesh axis runs over, the one named last changes fastest.
Arguments:
- hidden_in: bfloat16 [4096, 4096], P('tok', 'tp'), may hold values from -6 to 6
- norm_gain: float32 [4096], replicated, may hold values from 0.5 to 9, as said below
- w_query: bfloat16 [4096, 4096], P(None, 'tp'), may hold values from -0.09375 to 0.09375
- w_key: bfloat16 [4096, 1024], P(None, 'tp'), may hold values from -0.09375 to 0.09375
- w_value: bfloat16 [4096, 1024], P(None, 'tp'), may hold values from -0.09375 to 0.09375
- w_out: bfloat16 [4096, 4096], P('tp'), may hold values from -0.5 to 0.5
- doc_ids: int32 [4096], replicated, may hold values from 0 to 3, never falling along the last dimension, each value on 1 to 3072 neighbouring positions
Outputs:
- hidden_out: bfloat16 [4096, 4096], P('tok', 'tp')
- joint_cov: float32 [2, 4096, 2, 4096], P(None, 'tok', None, 'tp')
Inputs may be any that keep to these rules, and one draw needn't show every extreme that they name: `norm_gain`: each channel's gain is positive. `doc_ids`: document numbers never fall along the tokens; a document holds 1 to 3072 tokens.
All inputs are finite; a program needn't handle non-finite values.
Results may differ from a plain program's by a relative error of at most 0.013.
The roundings to bfloat16 on the way count: a program that leaves them out, or rounds other values in their place, can miss the bound.
Values may be sent and summed in bfloat16 or wider, within the bound.
A program may use at most 192 MiB of HBM per device.

v0:
```python
import functools
import math

import jax
import jax.numpy as jnp
from jax import lax
from jax.experimental import pallas as pl
from jax.experimental.pallas import tpu as pltpu
from jax.sharding import PartitionSpec as P

HS = 128
epsilon = 1e-05
rope_base = 500000.0
VMEM_LIMIT = 60 * 1024 * 1024


def rotate(vectors, positions):
    half_dim = vectors.shape[-1] // 2
    inv_freq = rope_base ** (-(jnp.arange(half_dim, dtype=jnp.float32) * 2.0) / vectors.shape[-1])
    angles = positions.astype(jnp.float32)[:, None] * inv_freq[None, :]
    cosine = jnp.cos(angles)[:, None, :]
    sine_part = jnp.sin(angles)[:, None, :]
    first_half = vectors[..., :half_dim]
    second_half = vectors[..., half_dim:]
    return jnp.concatenate(
        [
            first_half * cosine - second_half * sine_part,
            second_half * cosine + first_half * sine_part,
        ],
        axis=-1,
    )


def attend_kernel(groups, block, bounds, q_ref, k_ref, v_ref, lo_ref, out_ref, s_ref, m_ref, l_ref, acc_ref):
    rows = q_ref.shape[0]
    first_row = bounds[0]
    scale = HS ** (-0.5) * math.log2(math.e)
    start = bounds[1] // block
    stop = (first_row + rows + block - 1) // block
    lanes = 128
    m_ref[...] = jnp.full_like(m_ref, -jnp.inf)
    l_ref[...] = jnp.zeros_like(l_ref)
    acc_ref[...] = jnp.zeros_like(acc_ref)

    @pl.loop(start, stop)
    def _(step):
        first_key = pl.multiple_of(step * block, block)
        keys = k_ref[pl.ds(first_key, block), :]
        key_pos = first_key + lax.broadcasted_iota(jnp.int32, (rows, block), 1)
        query_pos = first_row + lax.broadcasted_iota(jnp.int32, (rows, block), 0)
        allowed = (key_pos >= lo_ref[:, :1]) & (key_pos <= query_pos)
        for head in range(groups):
            part = pl.ds(head * rows, rows)
            s = lax.dot_general(
                q_ref[:, head * HS:(head + 1) * HS], keys,
                (((1,), (1,)), ((), ())), preferred_element_type=jnp.float32,
            ) * scale
            s = jnp.where(allowed, s, -jnp.inf)
            s_ref[step, part, :] = s
            top = m_ref[part, :]
            for piece in range(block // lanes):
                top = jnp.maximum(top, s[:, piece * lanes:(piece + 1) * lanes])
            m_ref[part, :] = top

    m_ref[...] = jnp.broadcast_to(jnp.max(m_ref[...], axis=-1, keepdims=True), m_ref.shape)

    @pl.loop(start, stop)
    def _(step):
        first_key = pl.multiple_of(step * block, block)
        values = v_ref[pl.ds(first_key, block), :]
        for head in range(groups):
            part = pl.ds(head * rows, rows)
            weights = jnp.exp2(s_ref[step, part, :] - m_ref[part, :1])
            total = l_ref[part, :]
            for piece in range(block // lanes):
                total = total + weights[:, piece * lanes:(piece + 1) * lanes]
            l_ref[part, :] = total
            acc_ref[part, :] += jnp.dot(
                weights.astype(jnp.bfloat16), values, preferred_element_type=jnp.float32
            )

    for head in range(groups):
        part = pl.ds(head * rows, rows)
        weight_sum = jnp.sum(l_ref[part, :], axis=-1, keepdims=True)
        out_ref[:, head * HS:(head + 1) * HS] = (acc_ref[part, :] / weight_sum).astype(out_ref.dtype)


def attend(queries, kv_rows, lo, bounds, kv_heads):
    rows, width = queries.shape
    all_rows = kv_rows.shape[1]
    groups = width // (kv_heads * HS)
    block = min(512, all_rows)
    wide = groups * HS
    return pl.pallas_call(
        functools.partial(attend_kernel, groups, block),
        out_shape=jax.ShapeDtypeStruct((rows, width), jnp.bfloat16),
        grid_spec=pltpu.PrefetchScalarGridSpec(
            num_scalar_prefetch=1,
            grid=(kv_heads,),
            in_specs=[
                pl.BlockSpec((rows, wide), lambda g, b: (0, g)),
                pl.BlockSpec((None, all_rows, HS), lambda g, b: (0, 0, g)),
                pl.BlockSpec((None, all_rows, HS), lambda g, b: (1, 0, g)),
                pl.BlockSpec((rows, 128), lambda g, b: (0, 0)),
            ],
            out_specs=pl.BlockSpec((rows, wide), lambda g, b: (0, g)),
            scratch_shapes=[
                pltpu.VMEM((all_rows // block, groups * rows, block), jnp.float32),
                pltpu.VMEM((groups * rows, 128), jnp.float32),
                pltpu.VMEM((groups * rows, 128), jnp.float32),
                pltpu.VMEM((groups * rows, HS), jnp.float32),
            ],
        ),
        compiler_params=pltpu.CompilerParams(
            dimension_semantics=("arbitrary",), vmem_limit_bytes=VMEM_LIMIT
        ),
        cost_estimate=pl.CostEstimate(
            flops=4 * rows * all_rows * width,
            bytes_accessed=2 * all_rows * kv_heads * HS * 2 + 4 * rows * width,
            transcendentals=rows * all_rows * width // HS,
        ),
        name="attend",
    )(bounds, queries, kv_rows, kv_rows, lo)


def gram_kernel(strips, rin_ref, rout_ref, low_ref, high_ref, cout_ref, out_ref, rt_ref, mean_ref):
    all_rows, row_width = rin_ref.shape

    @pl.when(pl.program_id(0) == 0)
    def _():
        ones = jnp.ones((all_rows, 128), jnp.bfloat16)
        for source, ref in enumerate((rin_ref, rout_ref)):
            part = pl.ds(source * row_width, row_width)
            rt_ref[part, :] = ref[...].T
            mean_ref[part, :] = (
                jnp.dot(rt_ref[part, :], ones, preferred_element_type=jnp.float32) / all_rows
            )

    ones = jnp.ones((8, all_rows), jnp.bfloat16)

    def block(source, ref):
        cols = ref[...]
        col_mean = jnp.dot(ones, cols, preferred_element_type=jnp.float32)[:1] / all_rows
        gram = jnp.dot(rt_ref[...], cols, preferred_element_type=jnp.float32)
        cov = gram / all_rows - mean_ref[:, :1] * col_mean
        for row_source in range(2):
            out_ref[row_source, :, source, :] = cov[row_source * row_width:(row_source + 1) * row_width]

    @pl.when(pl.program_id(0) < strips)
    def _():
        block(0, low_ref)

    @pl.when(pl.program_id(0) >= strips)
    def _():
        block(0, high_ref)

    block(1, cout_ref)


def joint_gram(rin, rout, cin, cout):
    all_rows, row_width = rin.shape
    half = cout.shape[2]
    col_width = 2 * half
    tile = min(256, half)
    strips = half // tile
    whole = pl.BlockSpec((all_rows, row_width), lambda j: (0, 0), pipeline_mode=pl.Buffered(1))
    strip = pl.BlockSpec((None, all_rows, tile), lambda j: (j // strips, 0, j % strips))
    low = pl.BlockSpec((all_rows, tile), lambda j: (0, jnp.minimum(j, strips - 1)))
    high = pl.BlockSpec((all_rows, tile), lambda j: (0, jnp.maximum(j - strips, 0)))
    return pl.pallas_call(
        functools.partial(gram_kernel, strips),
        out_shape=jax.ShapeDtypeStruct((2, row_width, 2, col_width), jnp.float32),
        grid=(col_width // tile,),
        in_specs=[whole, whole, low, high, strip],
        out_specs=pl.BlockSpec((2, row_width, 2, tile), lambda j: (0, 0, 0, j)),
        scratch_shapes=[
            pltpu.VMEM((2 * row_width, all_rows), jnp.bfloat16),
            pltpu.VMEM((2 * row_width, 128), jnp.float32),
        ],
        compiler_params=pltpu.CompilerParams(
            dimension_semantics=("arbitrary",), vmem_limit_bytes=VMEM_LIMIT
        ),
        cost_estimate=pl.CostEstimate(
            flops=8 * all_rows * row_width * col_width,
            bytes_accessed=4 * all_rows * (row_width + col_width) + 16 * row_width * col_width,
            transcendentals=0,
        ),
        name="joint_gram",
    )(rin, rout, *cin, cout)


def both_sides(block):
    if lax.axis_size("tp") != 2:
        return lax.all_gather(block, "tp", axis=1, tiled=True)
    other = lax.ppermute(block, "tp", ((0, 1), (1, 0)))
    first = lax.axis_index("tp") == 0
    return jnp.concatenate([jnp.where(first, block, other), jnp.where(first, other, block)], axis=1)


def ring_kernel(chips, share, x_ref, *refs):
    if share:
        out_ref, side_ref, send, recv, psend, precv, local, ssend, srecv = refs
    else:
        out_ref, send, recv, psend, precv, local = refs
    mesh_id = pl.DeviceIdType.MESH
    rows = x_ref.shape[1]
    me, tp = lax.axis_index("tok"), lax.axis_index("tp")
    count = 2 * chips
    core, chip = me % 2, me // 2
    depth = chips // 2
    spot = jnp.where(chip % 2 == 0, chip // 2, chips - 1 - chip // 2)

    def device(place):
        place = (place + 2 * chips) % chips
        return jnp.where(place < depth, place * 4, (chips - 1 - place) * 4 + 2) + core

    partner = me + 1 - 2 * core
    ways = (device(spot + 1), device(spot - 1))
    barrier = pltpu.get_barrier_semaphore()
    for peer in (*ways, partner):
        pl.semaphore_signal(barrier, inc=1, device_id={"tok": peer}, device_id_type=mesh_id)
    if share:
        pl.semaphore_signal(barrier, inc=1, device_id={"tp": 1 - tp}, device_id_type=mesh_id)
    pl.semaphore_wait(barrier, 4 if share else 3)

    def block(way, origin):
        return out_ref.at[way, pl.ds(pl.multiple_of(origin * rows, rows), rows), :]

    pending = []

    def step_copies(step, way):
        origin = device(spot - step if way == 0 else spot + step)
        source = x_ref.at[way] if step == 0 else block(way, origin)
        ring = None
        if step < chips - 1:
            ring = pltpu.make_async_remote_copy(
                src_ref=source, dst_ref=block(way, origin), send_sem=send.at[way, step],
                recv_sem=recv.at[way, step], device_id={"tok": ways[way]}, device_id_type=mesh_id,
            )
            ring.start()
        beside = pltpu.make_async_remote_copy(
            src_ref=source, dst_ref=block(way, origin), send_sem=psend.at[way, step],
            recv_sem=precv.at[way, step], device_id={"tok": partner}, device_id_type=mesh_id,
        )
        beside.start()
        pending.append((ring, beside))
        return ring

    rings = [step_copies(0, way) for way in range(2)]
    own = [pltpu.make_async_copy(x_ref.at[way], block(way, me), local.at[way]) for way in range(2)]
    for copy in own:
        copy.start()
    if share:
        width = side_ref.shape[1]
        half = x_ref.shape[2]
        owner = me // (count // 2)
        my_way = me * width % (2 * half) // half
        features = pl.ds(pl.multiple_of(me * width % half, width), width)

    def side_copy(step, way, kind):
        origin = device(spot - step if way == 0 else spot + step)
        origin = origin + kind * (1 - 2 * core)
        source = x_ref.at[way, :, features]
        if step > 0 or kind > 0:
            source = out_ref.at[way, pl.ds(pl.multiple_of(origin * rows, rows), rows), features]
        return pltpu.make_async_remote_copy(
            src_ref=source,
            dst_ref=side_ref.at[pl.ds(pl.multiple_of(origin * rows, rows), rows), :],
            send_sem=ssend.at[kind, step], recv_sem=srecv.at[kind, step],
            device_id={"tp": 1 - tp}, device_id_type=mesh_id,
        )

    def each_side(act, step, way, kind, holder):
        if share:
            @pl.when((my_way == way) & ((owner == tp) == holder))
            def _():
                act(side_copy(step, way, kind))

    def start(copy):
        copy.start()

    for way in range(2):
        each_side(start, 0, way, 0, True)
    for step in range(1, chips):
        for way in range(2):
            rings[way].wait_recv()
            rings[way] = step_copies(step, way)
            each_side(start, step, way, 0, True)
            pending[2 * (step - 1) + way][1].wait_recv()
            each_side(start, step - 1, way, 1, True)
    for way in range(2):
        pending[2 * (chips - 1) + way][1].wait_recv()
        each_side(start, chips - 1, way, 1, True)
    for ring, beside in pending:
        if ring is not None:
            ring.wait_send()
        beside.wait_send()
    for copy in own:
        copy.wait()
    for step in range(chips):
        for way in range(2):
            for kind in range(2):
                each_side(lambda copy: copy.wait_send(), step, way, kind, True)
                each_side(lambda copy: copy.wait_recv(), step, way, kind, False)


def ring_gather(halves, share, call_id):
    _, rows, width = halves.shape
    count = lax.axis_size("tok")
    chips = count // 2
    out_shape = [jax.ShapeDtypeStruct((2, rows * count, width), halves.dtype)]
    dma = pltpu.SemaphoreType.DMA
    scratch = [dma((2, chips))] * 4 + [dma((2,))]
    if share:
        out_shape.append(jax.ShapeDtypeStruct((rows * count, 4 * width // count), halves.dtype))
        scratch += [dma((2, chips))] * 2
    return pl.pallas_call(
        functools.partial(ring_kernel, chips, share),
        out_shape=out_shape,
        in_specs=[pl.BlockSpec(memory_space=pltpu.VMEM)],
        out_specs=[pl.BlockSpec(memory_space=pl.ANY)] * len(out_shape),
        scratch_shapes=scratch,
        compiler_params=pltpu.CompilerParams(
            collective_id=call_id, has_side_effects=True, vmem_limit_bytes=VMEM_LIMIT
        ),
        cost_estimate=pl.CostEstimate(
            flops=40_000_000_000, bytes_accessed=2 * halves.size * count * 2, transcendentals=0
        ),
        name="ring_share" if share else "ring",
    )(halves)


def row_features(columns, arrived):
    _, all_rows, half = columns.shape
    row_width = 2 * half * lax.axis_size("tp") // lax.axis_size("tok")
    first = lax.axis_index("tok") * row_width
    offset, owner = first % (2 * half), first // (2 * half)
    mine = lax.dynamic_slice(columns, (offset // half, 0, offset % half), (1, all_rows, row_width))[0]
    owned = lax.axis_index("tp") == owner
    if arrived is None:
        return lax.psum(jnp.where(owned, mine, jnp.zeros_like(mine)), "tp")
    return jnp.where(owned, mine, arrived)


def on_device(hidden_in, norm_gain, w_query, w_key, w_value, w_out, doc_ids):
    tok_rows, col_width = hidden_in.shape
    tok_count = lax.axis_size("tok")
    tp_count = lax.axis_size("tp")
    tok_index = lax.axis_index("tok")
    all_rows = tok_rows * tok_count
    full_in = both_sides(hidden_in)
    widened = full_in.astype(jnp.float32)
    factor = lax.rsqrt(jnp.mean(widened * widened, axis=1, keepdims=True) + epsilon)
    normed = (widened * factor * norm_gain[None, :]).astype(jnp.bfloat16)
    kv_heads = w_key.shape[1] // HS
    groups = w_query.shape[1] // w_key.shape[1]
    first_row = tok_index * tok_rows
    positions = first_row + jnp.arange(tok_rows, dtype=jnp.int32)
    key_local = rotate(
        jnp.dot(normed, w_key, preferred_element_type=jnp.float32).reshape(tok_rows, kv_heads, HS),
        positions % all_rows,
    )
    key_local = key_local.astype(jnp.bfloat16).reshape(tok_rows, kv_heads * HS)
    value_local = jnp.dot(normed, w_value, preferred_element_type=jnp.float32).astype(jnp.bfloat16)
    (kv_rows,) = ring_gather(jnp.stack([key_local, value_local]), False, 0)
    early, late = hidden_in[:, : col_width // 2], hidden_in[:, col_width // 2 :]
    late, kv_rows = lax.optimization_barrier((late, kv_rows))
    cols_in = [lax.all_gather(part, "tok", axis=0, tiled=True) for part in (early, late)]
    rows_in = lax.all_to_all(full_in, "tok", 1, 0, tiled=True)
    queries = rotate(
        jnp.dot(normed, w_query, preferred_element_type=jnp.float32).reshape(
            tok_rows, kv_heads * groups, HS
        ),
        positions % all_rows,
    )
    queries = queries.astype(jnp.bfloat16).reshape(tok_rows, kv_heads * groups * HS)
    query_doc = lax.dynamic_slice_in_dim(doc_ids, first_row, tok_rows, 0)
    lo = jnp.sum((doc_ids[None, :] < query_doc[:, None]).astype(jnp.int32), axis=1)
    bounds = jnp.stack([first_row.astype(jnp.int32), lo[0]])
    attended = attend(queries, kv_rows, jnp.broadcast_to(lo[:, None], (tok_rows, 128)), bounds, kv_heads)
    partial_out = jnp.dot(attended, w_out, preferred_element_type=jnp.float32)
    if tp_count == 2:
        first = lax.axis_index("tp") == 0
        low, high = partial_out[:, :col_width], partial_out[:, col_width:]
        sent = jnp.where(first, high, low).astype(jnp.bfloat16)
        arrived = lax.ppermute(sent, "tp", ((0, 1), (1, 0)))
        summed = jnp.where(first, low, high) + arrived.astype(jnp.float32)
    else:
        summed = lax.psum_scatter(partial_out, "tp", scatter_dimension=1, tiled=True)
    hidden_out = (hidden_in.astype(jnp.float32) + summed).astype(jnp.bfloat16)
    halves = jnp.stack([hidden_out[:, : col_width // 2], hidden_out[:, col_width // 2 :]])
    if tp_count == 2:
        cols_out, arrived_rows = ring_gather(halves, True, 1)
        rows_out = row_features(cols_out, arrived_rows)
    else:
        (cols_out,) = ring_gather(halves, False, 1)
        rows_out = row_features(cols_out, None)
    return (hidden_out, joint_gram(rows_in, rows_out, cols_in, cols_out))


def solution(mesh):
    return jax.shard_map(
        on_device,
        mesh=mesh,
        in_specs=(
            P("tok", "tp"),
            P(),
            P(None, "tp"),
            P(None, "tp"),
            P(None, "tp"),
            P("tp", None),
            P(),
        ),
        out_specs=(P("tok", "tp"), P(None, "tok", None, "tp")),
        check_vma=False,
    )
```

profile of v0, /device:TPU:0, one launch (start us, length us, event | category | flops | bytes accessed | tf_op | source)
XLA Modules:
  0.0 380.6 jit_solution(14503733692742604877)
XLA Ops:
  7.2 2.2 fusion.10
  9.5 3.0 collective-permute-start
  13.1 22.9 %collective-permute-done = bf16[256,2048]{1,0:T(8,128)(2,1)} collective-permute-done((bf16[256,2048]{1,0:T(8,128)(2,1)}, bf16[256,2048]{1,0:T(8,128)(2,1)}, u32[]{:S(2)}, u32[]{:S(2)}) %collective-permute-start) | collective-permute-done | bytes 1048608 | tf_op jit(solution)/shard_map/ppermute | solution.py:195
  36.0 1.7 broadcast_select_fusion.1
  38.2 1.3 fusion.7
  40.7 3.5 fusion.3
  44.2 0.8 pad_maximum_fusion.3.x_ref
  45.1 85.2 %ring.1.k_ref.v_ref = bf16[2,4096,512]{2,1,0:T(8,128)(2,1)} custom-call(bf16[2,256,512]{2,1,0:T(8,128)(2,1)} %pad_maximum_fusion.3.x_ref), custom_call_target="tpu_custom_call" | custom-call | flops 40000000000 | bytes 16777216 | tf_op jit(solution)/shard_map/ring/pallas_call | solution.py:317
  131.5 1.3 pad_add_fusion.bounds
  132.7 8.6 %convolution_bitcast_fusion = f32[32,8,16,128]{3,1,2,0:T(8,128)S(1)} fusion(bf16[4096,2048]{1,0:T(8,128)(2,1)} %param.9, f32[4096]{0:T(1024)S(1)} %copy-done.5, f32[256]{0:T(256)S(1)} %add_rsqrt_fusion, bf16[256,2048]{1,0:T(8,128)(2,1)S(1)} %get-tuple-element.13, bf16[256,2048]{1,0:T(8,128)(2,1)S(1)} %get-tuple-element.12), kind=kOutput, calls=%fused_computation.13 | convolution fusion | flops 4302307328 | bytes 20988928 | tf_op jit(solution)/shard_map/dot_general | solution.py:371
  141.7 0.8 subtract_convert_fusion
  143.1 1.2 copy.17
  144.3 0.8 broadcast_in_dim.2.lo_ref
  145.1 10.1 %attend.1 = bf16[256,2048]{1,0:T(8,128)(2,1)} custom-call(s32[2]{0:T(128)} %pad_add_fusion.bounds, bf16[256,2048]{1,0:T(8,128)(2,1)} %bitcast.31, bf16[2,4096,512]{2,1,0:T(8,128)(2,1)} %ring.1.k_ref.v_ref, bf16[2,4096,512]{2,1,0:T(8,128)(2,1)} %ring.1.k_ref.v_ref, s32[256,128]{1,0:T(8,128)} %broadcast_in_dim.2.lo_ref), custom_call_target="tpu_custom_call" | custom-call | flops 8589934592 | bytes 10485760 | tf_op jit(solution)/shard_map/attend/pallas_call | solution.py:94
  155.2 8.4 %fusion.11 = f32[256,4096]{1,0:T(8,128)S(1)} fusion(bf16[256,2048]{1,0:T(8,128)(2,1)} %attend.1, bf16[2048,4096]{1,0:T(8,128)(2,1)} %param.12), kind=kOutput, calls=%fused_computation.39 | convolution fusion | flops 4294967296 | bytes 22020096 | tf_op jit(solution)/shard_map/dot_general | solution.py:381
  163.6 2.0 copy-done
  165.8 2.1 collective-permute-start.1
  168.1 1.5 copy.16
  169.6 23.4 %all-to-all-start = ((bf16[256,16,256]{2,0,1:T(8,128)(2,1)}), bf16[256,16,256]{2,0,1:T(8,128)(2,1)}, u32[]{:S(2)}, u32[]{:S(2)}) async-start(bf16[256,16,256]{2,0,1:T(8,128)(2,1)} %bitcast.26), calls=%async_computation | async-start | bytes 4194304 | tf_op jit(solution)/shard_map/all_to_all | solution.py:369
  193.1 3.2 add_convert_fusion
  196.4 1.2 pad_maximum_fusion.2.x_ref
  197.6 139.3 %ring_share.1 = (bf16[2,4096,1024]{2,1,0:T(8,128)(2,1)}, bf16[4096,256]{1,0:T(8,128)(2,1)}) custom-call(bf16[2,256,1024]{2,1,0:T(8,128)(2,1)} %pad_maximum_fusion.2.x_ref), custom_call_target="tpu_custom_call" | custom-call | flops 40000000000 | bytes 33554432 | tf_op jit(solution)/shard_map/ring_share/pallas_call | solution.py:317
  336.9 4.5 %bitcast_select_fusion.rout_ref = bf16[4096,256]{1,0:T(8,128)(2,1)} fusion(bf16[4096,256]{1,0:T(8,128)(2,1)} %get-tuple-element.8, bf16[2,4096,1024]{2,1,0:T(8,128)(2,1)} %get-tuple-element.7.cout_ref, s32[]{:T(128)S(6)} %select_n.80, s32[]{:T(128)S(6)} %select_n.82, pred[]{:T(512)S(6)} %eq.14), kind=kLoop, calls=%fused_computation.8 | loop fusion | flops 1048576 | bytes 6291465 | tf_op jit(solution)/shard_map/jit(_where)/select_n | solution.py:342
  341.4 32.3 %joint_gram.1 = f32[2,256,2,2048]{3,2,1,0:T(2,128)} custom-call(bf16[4096,256]{1,0:T(8,128)(2,1)} %bitcast.3.rin_ref, bf16[4096,256]{1,0:T(8,128)(2,1)} %bitcast_select_fusion.rout_ref, bf16[4096,1024]{1,0:T(8,128)(2,1)} %all-gather.3.cloned.1.call-done.low_ref, bf16[4096,1024]{1,0:T(8,128)(2,1)} %all-gather.5.cloned.1.call-done.high_ref, ...), custom_call_target="tpu_custom_call" | custom-call | flops 17179869184 | bytes 46137344 | tf_op jit(solution)/shard_map/joint_gram/pallas_call | solution.py:170
  (36 shorter events, 5.0 us)
Async XLA Ops:
  7.2 31.1 %copy-start.5 = (f32[4096]{0:T(1024)S(1)}, f32[4096]{0:T(1024)}, u32[]{:S(2)}) copy-start(f32[4096]{0:T(1024)} %param.8) | copy-start | bytes 49156
  7.2 334.2 %all-gather.3.cloned.1.call-start = ((), (), s32[]{:S(2)}) async-start(), calls=%async_computation.1 | async-start | bytes 8912896 | tf_op jit(solution)/shard_map/all_gather | solution.py:368
  9.5 331.9 %all-gather.5.cloned.1.call-start = ((), (), s32[]{:S(2)}) async-start(), calls=%async_computation.2 | async-start | bytes 8912896 | tf_op jit(solution)/shard_map/all_gather | solution.py:368
  9.5 26.5 %collective-permute-start = (bf16[256,2048]{1,0:T(8,128)(2,1)}, bf16[256,2048]{1,0:T(8,128)(2,1)}, u32[]{:S(2)}, u32[]{:S(2)}) collective-permute-start(bf16[256,2048]{1,0:T(8,128)(2,1)} %param.7), channel_id=1, source_target_pairs={{0,1},{1,0},{2,3},{3,2},{4,5},{5,4},{6,7},{7,6},{8,9},{9,8},{10,11... | collective-permute-start | bytes 3145736 | tf_op jit(solution)/shard_map/ppermute | solution.py:195
  12.6 25.7 %copy-start.4 = (bf16[4096,512]{1,0:T(8,128)(2,1)S(1)}, bf16[4096,512]{1,0:T(8,128)(2,1)}, u32[]{:S(2)}) copy-start(bf16[4096,512]{1,0:T(8,128)(2,1)} %param.10) | copy-start | bytes 12582916
  45.0 85.2 %copy-start.3 = (s32[4096]{0:T(1024)S(1)}, s32[4096]{0:T(1024)}, u32[]{:S(2)}) copy-start(s32[4096]{0:T(1024)} %param.13) | copy-start | bytes 49156
  163.6 2.0 copy-start
  165.8 27.3 %collective-permute-start.1 = (bf16[256,2048]{1,0:T(8,128)(2,1)S(1)}, bf16[256,2048]{1,0:T(8,128)(2,1)}, u32[]{:S(2)}, u32[]{:S(2)}) collective-permute-start(bf16[256,2048]{1,0:T(8,128)(2,1)S(1)} %select_convert_fusion), channel_id=1, source_target_pairs={{0,1},{1,0},{2,3},{3,2},{4,5},{5,4},{6,7},{7,6},{8,9},{9,8},{10,11... | collective-permute-start | bytes 3145736 | tf_op jit(solution)/shard_map/ppermute | solution.py:386
  168.1 25.0 %copy-start.1 = (bf16[256,2048]{1,0:T(8,128)(2,1)S(1)}, bf16[256,2048]{1,0:T(8,128)(2,1)}, u32[]{:S(2)}) copy-start(bf16[256,2048]{1,0:T(8,128)(2,1)} %param.7) | copy-start | bytes 3145732
  169.6 171.8 %all-to-all-start = ((bf16[256,16,256]{2,0,1:T(8,128)(2,1)}), bf16[256,16,256]{2,0,1:T(8,128)(2,1)}, u32[]{:S(2)}, u32[]{:S(2)}) async-start(bf16[256,16,256]{2,0,1:T(8,128)(2,1)} %bitcast.26), calls=%async_computation | async-start | bytes 4194304 | tf_op jit(solution)/shard_map/all_to_all | solution.py:369
  196.3 140.6 %copy-start.2 = (bf16[256,2048]{1,0:T(8,128)(2,1)}, bf16[256,2048]{1,0:T(8,128)(2,1)S(1)}, u32[]{:S(2)}) copy-start(bf16[256,2048]{1,0:T(8,128)(2,1)S(1)} %add_convert_fusion) | copy-start | bytes 3145732
Sparse Core Ops, SparseCore 0:
  10.1 92.3 all-gather.2
  130.4 88.4 all-gather.4
where the time goes:
time: 383 us; the launch traced here: 381 us
  Pallas kernels  267 us (70%)
  starting transfers between devices  28.6 us (7%)
  waiting for transfers between devices  23 us (6%)
  matrix products  21.8 us (6%)
  other arithmetic  17 us (4%)
  between operations  14.3 us (4%)
  local copies, waits for them, and re-layouts  9.14 us (2%)
    pallas_call x2, Pallas kernels, ring_gather(): pl.pallas_call(functools.partial(ring_kernel, chips, share), out_shape=ou...  224 us
    pallas_call x1, Pallas kernels, joint_gram(): pl.pallas_call(functools.partial(gram_kernel, strips), out_shape=jax.Shap...  32.3 us
    all_to_all x1, starting transfers between devices, on_device(): rows_in = lax.all_to_all(full_in, 'tok', 1, 0, tiled=True)  23.4 us
    ppermute x1, waiting for transfers between devices, both_sides(): other = lax.ppermute(block, 'tp', ((0, 1), (1, 0)))  22.9 us
    pallas_call x1, Pallas kernels, attend(): pl.pallas_call(functools.partial(attend_kernel, groups, block), out_shape...  10.1 us
    dot_general x1, matrix products, on_device(): jnp.dot(normed, w_query, preferred_element_type=jnp.float32)  8.57 us
    dot_general x1, matrix products, on_device(): partial_out = jnp.dot(attended, w_out, preferred_element_type=jnp.float32)  8.42 us
  transfers between devices with their start and end apart: 5, of which 1 were waited for; matrix products, arithmetic and copies ran while one was open for 11% of the time, Pallas kernels for 62%

commit v1 on v0

--- a/solution.py
+++ b/solution.py
@@ -340,6 +340,260 @@
     if arrived is None:
         return lax.psum(jnp.where(owned, mine, jnp.zeros_like(mine)), "tp")
     return jnp.where(owned, mine, arrived)
+
+
+SUBS = 2
+MESH = pl.DeviceIdType.MESH
+
+
+def ring_place(chips):
+    me, tp = lax.axis_index("tok"), lax.axis_index("tp")
+    core, chip = me % 2, me // 2
+    spot = jnp.where(chip % 2 == 0, chip // 2, chips - 1 - chip // 2)
+
+    def chip_at(place):
+        place = (place + 2 * chips) % chips
+        return jnp.where(place < chips // 2, place * 2, (chips - 1 - place) * 2 + 1)
+
+    ahead = 1 - 2 * core
+    return me, tp, core, spot, chip_at, ahead
+
+
+def cov_kernel(chips, x_ref, rin_ref, *refs):
+    parts = len(refs) - 17
+    cin_refs, refs = refs[:parts], refs[parts:]
+    acc_ref, rsum_ref, big, far, lt, cbuf = refs[:6]
+    send, recv, psend, precv, ssend, srecv, tsend, trecv, own_sem, cin_sem = refs[6:16]
+    (ones_r,) = refs[16:]
+    me, tp, core, spot, chip_at, ahead = ring_place(chips)
+    rows, width = x_ref.shape
+    side = rin_ref.shape[1]
+    sub_rows = rows // SUBS
+    partner = me + 1 - 2 * core
+    onward = chip_at(spot + ahead) * 2 + core
+    back = chip_at(spot - ahead) * 2 + core
+    owner = me * side // width == tp
+    feature = pl.multiple_of(me * side % width, side)
+    partner_feature = pl.multiple_of(partner * side % width, side)
+
+    barrier = pltpu.get_barrier_semaphore()
+    for peer in (onward, back, partner):
+        pl.semaphore_signal(barrier, inc=1, device_id={"tok": peer}, device_id_type=MESH)
+    for peer in (me, partner):
+        pl.semaphore_signal(
+            barrier, inc=1, device_id={"tok": peer, "tp": 1 - tp}, device_id_type=MESH
+        )
+
+    def block_row(step, mine):
+        turn = ahead if mine else -ahead
+        return pl.multiple_of(
+            (chip_at(spot - turn * step) * 2 + (core if mine else 1 - core)) * rows, rows
+        )
+
+    def span(step, sub):
+        return pl.ds(pl.multiple_of(block_row(step, True) + sub * sub_rows, sub_rows), sub_rows)
+
+    def source(step, sub):
+        return x_ref.at[pl.ds(sub * sub_rows, sub_rows)] if step == 0 else big.at[span(step, sub)]
+
+    def ring_copy(step, sub):
+        return pltpu.make_async_remote_copy(
+            src_ref=source(step, sub), dst_ref=big.at[span(step, sub)],
+            send_sem=send.at[step, sub], recv_sem=recv.at[step, sub],
+            device_id={"tok": onward}, device_id_type=MESH,
+        )
+
+    def beside_copy(step, sub):
+        return pltpu.make_async_remote_copy(
+            src_ref=source(step, sub), dst_ref=big.at[span(step, sub)],
+            send_sem=psend.at[step, sub], recv_sem=precv.at[step, sub],
+            device_id={"tok": partner}, device_id_type=MESH,
+        )
+
+    def side_copy(step, sub, same):
+        wanted, target = (feature, me) if same else (partner_feature, partner)
+        out_sem, in_sem = (ssend, srecv) if same else (tsend, trecv)
+        return pltpu.make_async_remote_copy(
+            src_ref=source(step, sub).at[:, pl.ds(wanted, side)], dst_ref=far.at[span(step, sub), :],
+            send_sem=out_sem.at[step, sub], recv_sem=in_sem.at[step, sub],
+            device_id={"tok": target, "tp": 1 - tp}, device_id_type=MESH,
+        )
+
+    def launch(step, sub):
+        if step < chips - 1:
+            ring_copy(step, sub).start()
+        beside_copy(step, sub).start()
+
+        @pl.when(owner)
+        def _():
+            for same in (True, False):
+                side_copy(step, sub, same).start()
+
+    def fetch(step, mine):
+        slot = step % 2 * 2 + (0 if mine else 1)
+        piece = width // parts
+        return [
+            pltpu.make_async_copy(
+                ref.at[pl.ds(block_row(step, mine), rows), :],
+                cbuf.at[slot, :, pl.ds(i * piece, piece)], cin_sem.at[slot, i],
+            )
+            for i, ref in enumerate(cin_refs)
+        ]
+
+    tile = min(512, width)
+
+    def compute(step, mine):
+        slot = step % 2 * 2 + (0 if mine else 1)
+        place = pl.ds(block_row(step, mine), rows)
+        lt[0:side, :] = rin_ref[place, :].T
+
+        @pl.when(owner)
+        def _():
+            lt[side:2 * side, :] = big[place, pl.ds(feature, side)].T
+
+        @pl.when(jnp.logical_not(owner))
+        def _():
+            lt[side:2 * side, :] = far[place, :].T
+
+        for copy in fetch(step, mine):
+            copy.wait()
+        rsum_ref[...] += jnp.dot(lt[0:2 * side, :], ones_r[...], preferred_element_type=jnp.float32)
+
+        @pl.loop(0, width // tile)
+        def _(i):
+            here = pl.ds(pl.multiple_of(i * tile, tile), tile)
+            acc_ref[:, here] += jnp.dot(
+                lt[...], cbuf[slot, :, here], preferred_element_type=jnp.float32
+            )
+            there = pl.ds(pl.multiple_of(width + i * tile, tile), tile)
+            acc_ref[:, there] += jnp.dot(
+                lt[...], big[place, here], preferred_element_type=jnp.float32
+            )
+
+    def arrive(step, mine):
+        if not mine:
+            for sub in range(SUBS):
+                beside_copy(step, sub).wait_recv()
+
+        @pl.when(jnp.logical_not(owner))
+        def _():
+            for sub in range(SUBS):
+                side_copy(step, sub, mine).wait_recv()
+
+    pl.semaphore_wait(barrier, 5)
+    for sub in range(SUBS):
+        launch(0, sub)
+    own = pltpu.make_async_copy(x_ref, big.at[pl.ds(pl.multiple_of(me * rows, rows), rows)], own_sem.at[0])
+    own.start()
+    for step in range(2):
+        for mine in (True, False):
+            for copy in fetch(step, mine):
+                copy.start()
+    ones_r[...] = jnp.ones_like(ones_r)
+    lt[2 * side:, :] = jnp.ones((lt.shape[0] - 2 * side, rows), lt.dtype)
+    acc_ref[...] = jnp.zeros_like(acc_ref)
+    rsum_ref[...] = jnp.zeros_like(rsum_ref)
+    own.wait()
+
+    def work(step, mine):
+        arrive(step, mine)
+        compute(step, mine)
+        if step + 2 < chips:
+            for copy in fetch(step + 2, mine):
+                copy.start()
+
+    for step in range(1, chips):
+        for sub in range(SUBS):
+            ring_copy(step - 1, sub).wait_recv()
+            launch(step, sub)
+            if sub == 0:
+                work(step - 1, True)
+            if sub == SUBS - 1:
+                work(step - 1, False)
+    work(chips - 1, True)
+    work(chips - 1, False)
+    for step in range(chips):
+        for sub in range(SUBS):
+            if step < chips - 1:
+                ring_copy(step, sub).wait_send()
+            beside_copy(step, sub).wait_send()
+
+            @pl.when(owner)
+            def _():
+                for same in (True, False):
+                    side_copy(step, sub, same).wait_send()
+
+
+def finish_kernel(all_rows, *refs):
+    rsum_ref, out_ref = refs[4:]
+    side = out_ref.shape[1]
+    for source in range(2):
+        acc_ref, csum_ref = refs[2 * source:2 * source + 2]
+        mean_col = csum_ref[0:1, :] / all_rows
+        for row_source in range(2):
+            part = slice(row_source * side, (row_source + 1) * side)
+            cov = acc_ref[part, :] / all_rows - (rsum_ref[part, :1] / all_rows) * mean_col
+            out_ref[row_source, :, source, :] = cov
+
+
+def joint_cov(hidden_out, rows_in, cols_in, call_id):
+    rows, width = hidden_out.shape
+    all_rows, side = rows_in.shape
+    chips = all_rows // rows // 2
+    parts = len(cols_in)
+    dma = pltpu.SemaphoreType.DMA
+    tall = 2 * side + 16
+    acc, rsum = pl.pallas_call(
+        functools.partial(cov_kernel, chips),
+        out_shape=[
+            jax.ShapeDtypeStruct((tall, 2 * width), jnp.float32),
+            jax.ShapeDtypeStruct((2 * side, 128), jnp.float32),
+        ],
+        in_specs=[pl.BlockSpec(memory_space=pltpu.VMEM)] * 2
+        + [pl.BlockSpec(memory_space=pl.ANY)] * parts,
+        out_specs=[pl.BlockSpec(memory_space=pltpu.VMEM)] * 2,
+        scratch_shapes=[
+            pltpu.VMEM((all_rows, width), jnp.bfloat16),
+            pltpu.VMEM((all_rows, side), jnp.bfloat16),
+            pltpu.VMEM((tall, rows), jnp.bfloat16),
+            pltpu.VMEM((4, rows, width), jnp.bfloat16),
+        ]
+        + [dma((chips, SUBS))] * 8
+        + [dma((1,)), dma((4, parts))]
+        + [pltpu.VMEM((rows, 128), jnp.bfloat16)],
+        compiler_params=pltpu.CompilerParams(
+            collective_id=call_id, has_side_effects=True, vmem_limit_bytes=VMEM_LIMIT
+        ),
+        cost_estimate=pl.CostEstimate(
+            flops=8 * all_rows * side * width * 4,
+            bytes_accessed=4 * all_rows * (side + width) + 16 * side * width,
+            transcendentals=0,
+        ),
+        name="cov_ring",
+    )(hidden_out, rows_in, *cols_in)
+    return finish(acc, rsum, all_rows, side, width)
+
+
+def finish(acc, rsum, all_rows, side, width):
+    tile = min(256, width)
+    strips = width // tile
+    specs = []
+    for source in range(2):
+        specs.append(pl.BlockSpec((2 * side, tile), lambda j, source=source: (0, source * strips + j)))
+        specs.append(
+            pl.BlockSpec((8, tile), lambda j, source=source: (2 * side // 8, source * strips + j))
+        )
+    return pl.pallas_call(
+        functools.partial(finish_kernel, all_rows),
+        out_shape=jax.ShapeDtypeStruct((2, side, 2, width), jnp.float32),
+        grid=(strips,),
+        in_specs=specs + [pl.BlockSpec((2 * side, 128), lambda j: (0, 0))],
+        out_specs=pl.BlockSpec((2, side, 2, tile), lambda j: (0, 0, 0, j)),
+        compiler_params=pltpu.CompilerParams(
+            dimension_semantics=("arbitrary",), vmem_limit_bytes=VMEM_LIMIT
+        ),
+        name="finish",
+    )(acc, acc, acc, acc, rsum)
 
 
 def on_device(hidden_in, norm_gain, w_query, w_key, w_value, w_out, doc_ids):
@@ -388,13 +642,11 @@
     else:
         summed = lax.psum_scatter(partial_out, "tp", scatter_dimension=1, tiled=True)
     hidden_out = (hidden_in.astype(jnp.float32) + summed).astype(jnp.bfloat16)
+    if tp_count == 2:
+        return (hidden_out, joint_cov(hidden_out, rows_in, cols_in, 1))
     halves = jnp.stack([hidden_out[:, : col_width // 2], hidden_out[:, col_width // 2 :]])
-    if tp_count == 2:
-        cols_out, arrived_rows = ring_gather(halves, True, 1)
-        rows_out = row_features(cols_out, arrived_rows)
-    else:
-        (cols_out,) = ring_gather(halves, False, 1)
-        rows_out = row_features(cols_out, None)
+    (cols_out,) = ring_gather(halves, False, 1)
+    rows_out = row_features(cols_out, None)
     return (hidden_out, joint_gram(rows_in, rows_out, cols_in, cols_out))
 
 

time: 383 us -> 354 us (0.924)
  waiting for transfers between devices: 23 us -> 89.2 us
  Pallas kernels: 267 us -> 203 us
  starting transfers between devices: 28.6 us -> 8.96 us
  other arithmetic: 17 us -> 9.57 us
    pallas_call x2 -> x1, Pallas kernels: 224 us -> 85.1 us  [ring_gather(): pl.pallas_call(functools.partial(ring_kernel, chips, share), out_shape=ou...]
    pallas_call x1 -> x2, Pallas kernels: 32.3 us -> 107 us  [the longest x1 96.7 us: joint_cov(): pl.pallas_call(functools.partial(cov_kernel, chips), out_shape=[jax.Shape...]
    all_gather x2, waiting for transfers between devices: 0.01 us -> 25.8 us  [on_device(): lax.all_gather(part, 'tok', axis=0, tiled=True)]
    ppermute x1, waiting for transfers between devices: 0.01 us -> 23.7 us  [on_device(): arrived = lax.ppermute(sent, 'tp', ((0, 1), (1, 0)))]
    all_to_all x1, starting transfers between devices: 23.4 us -> 3.99 us  [on_device(): rows_in = lax.all_to_all(full_in, 'tok', 1, 0, tiled=True)]
    all_to_all x1, waiting for transfers between devices: 0.01 us -> 16.8 us  [on_device(): rows_in = lax.all_to_all(full_in, 'tok', 1, 0, tiled=True)]
    select_n x1 -> x0, other arithmetic: 4.54 us -> none  [row_features(): return jnp.where(owned, mine, arrived)]
  transfers between devices with their start and end apart: 5 -> 5, of which waited for: 1 -> 4; matrix products, arithmetic and copies ran while one was open for 11% -> 10% of each run, Pallas kernels for 62% -> 27%
where the time goes in v1:
time: 354 us
  Pallas kernels  203 us (57%)
  waiting for transfers between devices  89.2 us (25%)
  matrix products  22 us (6%)
  between operations  14.2 us (4%)
  other arithmetic  9.57 us (3%)
  starting transfers between devices  8.96 us (3%)
  local copies, waits for them, and re-layouts  7.15 us (2%)
    pallas_call x1, Pallas kernels, joint_cov(): pl.pallas_call(functools.partial(cov_kernel, chips), out_shape=[jax.Shape...  96.7 us
    pallas_call x1, Pallas kernels, ring_gather(): pl.pallas_call(functools.partial(ring_kernel, chips, share), out_shape=ou...  85.1 us
    all_gather x2, waiting for transfers between devices, on_device(): lax.all_gather(part, 'tok', axis=0, tiled=True)  25.8 us
    ppermute x1, waiting for transfers between devices, on_device(): arrived = lax.ppermute(sent, 'tp', ((0, 1), (1, 0)))  23.7 us
    ppermute x1, waiting for transfers between devices, both_sides(): other = lax.ppermute(block, 'tp', ((0, 1), (1, 0)))  22.9 us
    all_to_all x1, waiting for transfers between devices, on_device(): rows_in = lax.all_to_all(full_in, 'tok', 1, 0, tiled=True)  16.8 us
    pallas_call x1, Pallas kernels, finish(): pl.pallas_call(functools.partial(finish_kernel, all_rows), out_shape=jax....  10.7 us
    pallas_call x1, Pallas kernels, attend(): pl.pallas_call(functools.partial(attend_kernel, groups, block), out_shape...  10.1 us
  transfers between devices with their start and end apart: 5, of which 4 were waited for; matrix products, arithmetic and copies ran while one was open for 10% of the time, Pallas kernels for 27%

profile of v1, /device:TPU:0, one launch (start us, length us, event | category | flops | bytes accessed | tf_op | source)
XLA Modules:
  0.0 353.7 jit_solution(11033579374124113354)
XLA Ops:
  7.2 2.3 fusion.10
  9.6 3.0 collective-permute-start
  13.2 22.9 %collective-permute-done = bf16[256,2048]{1,0:T(8,128)(2,1)} collective-permute-done((bf16[256,2048]{1,0:T(8,128)(2,1)}, bf16[256,2048]{1,0:T(8,128)(2,1)}, u32[]{:S(2)}, u32[]{:S(2)}) %collective-permute-start) | collective-permute-done | bytes 1048608 | tf_op jit(solution)/shard_map/ppermute | solution.py:195
  36.1 1.7 broadcast_select_fusion.1
  38.3 1.3 fusion.7
  40.8 3.5 fusion.3
  44.3 0.8 pad_maximum_fusion.2.x_ref
  45.1 85.1 %ring.1.k_ref.v_ref = bf16[2,4096,512]{2,1,0:T(8,128)(2,1)} custom-call(bf16[2,256,512]{2,1,0:T(8,128)(2,1)} %pad_maximum_fusion.2.x_ref), custom_call_target="tpu_custom_call" | custom-call | flops 40000000000 | bytes 16777216 | tf_op jit(solution)/shard_map/ring/pallas_call | solution.py:317
  131.4 1.3 pad_add_fusion.bounds
  132.8 1.5 copy.16
  134.3 8.7 %convolution_bitcast_fusion = f32[32,8,16,128]{3,1,2,0:T(8,128)S(1)} fusion(bf16[4096,2048]{1,0:T(8,128)(2,1)} %param.9, f32[4096]{0:T(1024)S(1)} %copy-done.4, f32[256]{0:T(256)S(1)} %add_rsqrt_fusion, bf16[256,2048]{1,0:T(8,128)(2,1)S(1)} %get-tuple-element.13, bf16[256,2048]{1,0:T(8,128)(2,1)S(1)} %get-tuple-element.12), kind=kOutput, calls=%fused_computation.12 | convolution fusion | flops 4302307328 | bytes 20988928 | tf_op jit(solution)/shard_map/dot_general | solution.py:625
  143.4 0.8 subtract_convert_fusion
  144.8 1.2 copy.17
  146.0 4.0 %all-to-all-start = ((bf16[256,16,256]{2,0,1:T(8,128)(2,1)}), bf16[256,16,256]{2,0,1:T(8,128)(2,1)S(1)}, u32[]{:S(2)}, u32[]{:S(2)}) async-start(bf16[256,16,256]{2,0,1:T(8,128)(2,1)} %bitcast.20), calls=%async_computation | async-start | bytes 4194304 | tf_op jit(solution)/shard_map/all_to_all | solution.py:623
  150.0 0.8 broadcast_in_dim.2.lo_ref
  150.8 10.1 %attend.1 = bf16[256,2048]{1,0:T(8,128)(2,1)} custom-call(s32[2]{0:T(128)} %pad_add_fusion.bounds, bf16[256,2048]{1,0:T(8,128)(2,1)} %bitcast.26, bf16[2,4096,512]{2,1,0:T(8,128)(2,1)} %ring.1.k_ref.v_ref, bf16[2,4096,512]{2,1,0:T(8,128)(2,1)} %ring.1.k_ref.v_ref, s32[256,128]{1,0:T(8,128)} %broadcast_in_dim.2.lo_ref), custom_call_target="tpu_custom_call" | custom-call | flops 8589934592 | bytes 10485760 | tf_op jit(solution)/shard_map/attend/pallas_call | solution.py:94
  160.9 8.5 %fusion.11 = f32[256,4096]{1,0:T(8,128)S(1)} fusion(bf16[256,2048]{1,0:T(8,128)(2,1)} %attend.1, bf16[2048,4096]{1,0:T(8,128)(2,1)} %param.12), kind=kOutput, calls=%fused_computation.35 | convolution fusion | flops 4294967296 | bytes 22020096 | tf_op jit(solution)/shard_map/dot_general | solution.py:635
  169.6 1.9 collective-permute-start.1
  171.5 23.7 %collective-permute-done.1 = bf16[256,2048]{1,0:T(8,128)(2,1)S(1)} collective-permute-done((bf16[256,2048]{1,0:T(8,128)(2,1)S(1)}, bf16[256,2048]{1,0:T(8,128)(2,1)S(1)}, u32[]{:S(2)}, u32[]{:S(2)}) %collective-permute-start.1) | collective-permute-done | bytes 1048608 | tf_op jit(solution)/shard_map/ppermute | solution.py:640
  195.1 1.6 add_convert_fusion.x_ref
  196.8 16.8 %all-to-all-done = bf16[256,16,256]{2,0,1:T(8,128)(2,1)S(1)} async-done(((bf16[256,16,256]{2,0,1:T(8,128)(2,1)}), bf16[256,16,256]{2,0,1:T(8,128)(2,1)S(1)}, u32[]{:S(2)}, u32[]{:S(2)}) %all-to-all-start) | async-done | bytes 2097184 | tf_op jit(solution)/shard_map/all_to_all | solution.py:623
  213.5 25.8 %all-gather.5.cloned.1.call-done.refs_1_ = bf16[4096,1024]{1,0:T(8,128)(2,1)} async-done(((bf16[256,1024]{1,0:T(8,128)(2,1)}), bf16[4096,1024]{1,0:T(8,128)(2,1)}) %all-gather.5.cloned.1.call-update) | async-done | bytes 8388624 | tf_op jit(solution)/shard_map/all_gather | solution.py:622
  239.4 96.7 %cov_ring.1 = (f32[528,4096]{1,0:T(8,128)}, f32[512,128]{1,0:T(8,128)}) custom-call(bf16[256,2048]{1,0:T(8,128)(2,1)} %add_convert_fusion.x_ref, bf16[4096,256]{1,0:T(8,128)(2,1)} %bitcast.25, bf16[4096,1024]{1,0:T(8,128)(2,1)} %all-gather.3.cloned.1.call-done.refs_0_, bf16[4096,1024]{1,0:T(8,128)(2,1)} %all-gather.5.cloned.1.call-done.refs_1_), custom_call_target="tpu_custom_call" | custom-call | flops 68719476736 | bytes 46137344 | tf_op jit(solution)/shard_map/cov_ring/pallas_call | solution.py:546
  336.1 10.7 %finish.1 = f32[2,256,2,2048]{3,2,1,0:T(2,128)} custom-call(f32[528,4096]{1,0:T(8,128)} %get-tuple-element.8.refs_0_.refs_1_.refs_2_.refs_3_, f32[528,4096]{1,0:T(8,128)} %get-tuple-element.8.refs_0_.refs_1_.refs_2_.refs_3_, f32[528,4096]{1,0:T(8,128)} %get-tuple-element.8.refs_0_.refs_1_.refs_2_.refs_3_, ...), custom_call_target="tpu_custom_call" | custom-call | tf_op jit(solution)/shard_map/finish/pallas_call | solution.py:586
  (31 shorter events, 4.8 us)
Async XLA Ops:
  7.2 31.2 %copy-start.4 = (f32[4096]{0:T(1024)S(1)}, f32[4096]{0:T(1024)}, u32[]{:S(2)}) copy-start(f32[4096]{0:T(1024)} %param.8) | copy-start | bytes 49156
  7.2 206.4 %all-gather.3.cloned.1.call-start = ((), (), s32[]{:S(2)}) async-start(), calls=%async_computation.1 | async-start | bytes 8912896 | tf_op jit(solution)/shard_map/all_gather | solution.py:622
  9.6 229.8 %all-gather.5.cloned.1.call-start = ((), (), s32[]{:S(2)}) async-start(), calls=%async_computation.2 | async-start | bytes 8912896 | tf_op jit(solution)/shard_map/all_gather | solution.py:622
  9.6 26.5 %collective-permute-start = (bf16[256,2048]{1,0:T(8,128)(2,1)}, bf16[256,2048]{1,0:T(8,128)(2,1)}, u32[]{:S(2)}, u32[]{:S(2)}) collective-permute-start(bf16[256,2048]{1,0:T(8,128)(2,1)} %param.7), channel_id=1, source_target_pairs={{0,1},{1,0},{2,3},{3,2},{4,5},{5,4},{6,7},{7,6},{8,9},{9,8},{10,11... | collective-permute-start | bytes 3145736 | tf_op jit(solution)/shard_map/ppermute | solution.py:195
  12.7 25.7 %copy-start.3 = (bf16[4096,512]{1,0:T(8,128)(2,1)S(1)}, bf16[4096,512]{1,0:T(8,128)(2,1)}, u32[]{:S(2)}) copy-start(bf16[4096,512]{1,0:T(8,128)(2,1)} %param.10) | copy-start | bytes 12582916
  45.1 85.1 %copy-start.2 = (s32[4096]{0:T(1024)S(1)}, s32[4096]{0:T(1024)}, u32[]{:S(2)}) copy-start(s32[4096]{0:T(1024)} %param.13) | copy-start | bytes 49156
  146.0 67.5 %all-to-all-start = ((bf16[256,16,256]{2,0,1:T(8,128)(2,1)}), bf16[256,16,256]{2,0,1:T(8,128)(2,1)S(1)}, u32[]{:S(2)}, u32[]{:S(2)}) async-start(bf16[256,16,256]{2,0,1:T(8,128)(2,1)} %bitcast.20), calls=%async_computation | async-start | bytes 4194304 | tf_op jit(solution)/shard_map/all_to_all | solution.py:623
  160.9 34.2 %copy-start = (bf16[256,2048]{1,0:T(8,128)(2,1)S(1)}, bf16[256,2048]{1,0:T(8,128)(2,1)}, u32[]{:S(2)}) copy-start(bf16[256,2048]{1,0:T(8,128)(2,1)} %param.7) | copy-start | bytes 3145732
  169.6 25.5 %collective-permute-start.1 = (bf16[256,2048]{1,0:T(8,128)(2,1)S(1)}, bf16[256,2048]{1,0:T(8,128)(2,1)S(1)}, u32[]{:S(2)}, u32[]{:S(2)}) collective-permute-start(bf16[256,2048]{1,0:T(8,128)(2,1)S(1)} %select_convert_fusion), channel_id=1, source_target_pairs={{0,1},{1,0},{2,3},{3,2},{4,5},{5,4},{6,7},{7,6},{8,9},{9,8},{10,11... | collective-permute-start | bytes 3145736 | tf_op jit(solution)/shard_map/ppermute | solution.py:640
  213.5 25.8 %copy-start.1 = (bf16[256,16,256]{2,0,1:T(8,128)(2,1)}, bf16[256,16,256]{2,0,1:T(8,128)(2,1)S(1)}, u32[]{:S(2)}) copy-start(bf16[256,16,256]{2,0,1:T(8,128)(2,1)S(1)} %all-to-all-done) | copy-start | bytes 6291460
Sparse Core Ops, SparseCore 0:
  10.1 92.4 all-gather.2
  130.3 108.9 all-gather.4

commit v2 on v0

--- a/solution.py
+++ b/solution.py
@@ -342,10 +342,621 @@
     return jnp.where(owned, mine, arrived)
 
 
+SUBS = 2
+MESH = pl.DeviceIdType.MESH
+
+
+def ring_place(chips):
+    me, tp = lax.axis_index("tok"), lax.axis_index("tp")
+    core, chip = me % 2, me // 2
+    spot = jnp.where(chip % 2 == 0, chip // 2, chips - 1 - chip // 2)
+
+    def chip_at(place):
+        place = (place + 2 * chips) % chips
+        return jnp.where(place < chips // 2, place * 2, (chips - 1 - place) * 2 + 1)
+
+    ahead = 1 - 2 * core
+    return me, tp, core, spot, chip_at, ahead, chips
+
+
+class Ring:
+    def __init__(self, place, big, own, subs, sems, far=None, side=None, side_sems=None):
+        self.me, self.tp, self.core, self.spot, self.chip_at, self.ahead, self.chips = place
+        self.big, self.own, self.subs = big, own, subs
+        self.rows = big.shape[0] // (2 * self.chips)
+        self.part = self.rows // subs
+        self.send, self.recv, self.psend, self.precv = sems
+        self.far, self.side = far, side
+        self.partner = self.me + 1 - 2 * self.core
+        self.onward = self.chip_at(self.spot + self.ahead) * 2 + self.core
+        self.back = self.chip_at(self.spot - self.ahead) * 2 + self.core
+        if far is not None:
+            self.ssend, self.srecv, self.tsend, self.trecv = side_sems
+            width = big.shape[1]
+            self.owner = self.me * side // width == self.tp
+            self.feature = pl.multiple_of(self.me * side % width, side)
+            self.partner_feature = pl.multiple_of(self.partner * side % width, side)
+
+    def block(self, step, mine):
+        turn = self.ahead if mine else -self.ahead
+        return self.chip_at(self.spot - turn * step) * 2 + (self.core if mine else 1 - self.core)
+
+    def block_row(self, step, mine):
+        return pl.multiple_of(self.block(step, mine) * self.rows, self.rows)
+
+    def span(self, step, sub):
+        return pl.ds(pl.multiple_of(self.block_row(step, True) + sub * self.part, self.part), self.part)
+
+    def source(self, step, sub):
+        if self.own is not None and isinstance(step, int) and step == 0:
+            return self.own.at[pl.ds(sub * self.part, self.part)]
+        return self.big.at[self.span(step, sub)]
+
+    def ring_copy(self, step, sub):
+        return pltpu.make_async_remote_copy(
+            src_ref=self.source(step, sub), dst_ref=self.big.at[self.span(step, sub)],
+            send_sem=self.send.at[step, sub], recv_sem=self.recv.at[step, sub],
+            device_id={"tok": self.onward}, device_id_type=MESH,
+        )
+
+    def beside_copy(self, step, sub):
+        return pltpu.make_async_remote_copy(
+            src_ref=self.source(step, sub), dst_ref=self.big.at[self.span(step, sub)],
+            send_sem=self.psend.at[step, sub], recv_sem=self.precv.at[step, sub],
+            device_id={"tok": self.partner}, device_id_type=MESH,
+        )
+
+    def side_copy(self, step, sub, same):
+        wanted, target = (self.feature, self.me) if same else (self.partner_feature, self.partner)
+        out_sem, in_sem = (self.ssend, self.srecv) if same else (self.tsend, self.trecv)
+        return pltpu.make_async_remote_copy(
+            src_ref=self.source(step, sub).at[:, pl.ds(wanted, self.side)],
+            dst_ref=self.far.at[self.span(step, sub), :],
+            send_sem=out_sem.at[step, sub], recv_sem=in_sem.at[step, sub],
+            device_id={"tok": target, "tp": 1 - self.tp}, device_id_type=MESH,
+        )
+
+    def launch(self, step, sub):
+        if isinstance(step, int):
+            if step < self.chips - 1:
+                self.ring_copy(step, sub).start()
+        else:
+            @pl.when(step < self.chips - 1)
+            def _():
+                self.ring_copy(step, sub).start()
+        self.beside_copy(step, sub).start()
+
+    def launch_side(self, step, sub):
+        @pl.when(self.owner)
+        def _():
+            for same in (True, False):
+                self.side_copy(step, sub, same).start()
+
+    def event(self, step, sub):
+        self.ring_copy(step - 1, sub).wait_recv()
+        self.launch(step, sub)
+
+    def beside_arrived(self, step):
+        for sub in range(self.subs):
+            self.beside_copy(step, sub).wait_recv()
+
+    def side_arrived(self, step, mine):
+        @pl.when(jnp.logical_not(self.owner))
+        def _():
+            for sub in range(self.subs):
+                self.side_copy(step, sub, mine).wait_recv()
+
+    def drain(self):
+        for step in range(self.chips):
+            for sub in range(self.subs):
+                if step < self.chips - 1:
+                    self.ring_copy(step, sub).wait_send()
+                self.beside_copy(step, sub).wait_send()
+                if self.far is not None:
+                    @pl.when(self.owner)
+                    def _():
+                        for same in (True, False):
+                            self.side_copy(step, sub, same).wait_send()
+
+
+def greet(ring):
+    barrier = pltpu.get_barrier_semaphore()
+    for peer in (ring.onward, ring.back, ring.partner):
+        pl.semaphore_signal(barrier, inc=1, device_id={"tok": peer}, device_id_type=MESH)
+    for peer in (ring.me, ring.partner):
+        pl.semaphore_signal(
+            barrier, inc=1, device_id={"tok": peer, "tp": 1 - ring.tp}, device_id_type=MESH
+        )
+    pl.semaphore_wait(barrier, 5)
+
+
+def cov_kernel(chips, x_ref, cin_ref, rin_ref, *refs):
+    acc_ref, rsum_ref, big, far, lt, cbuf, rbuf = refs[:7]
+    sems, side_sems, own_sem, cin_sem, rin_sem, ones_r = refs[7:11], refs[11:15], *refs[15:]
+    ring = Ring(ring_place(chips), big, x_ref, SUBS, sems, far, rin_ref.shape[1], side_sems)
+    rows, width = x_ref.shape
+    side = ring.side
+    owner = ring.owner
+    greet(ring)
+    for sub in range(SUBS):
+        ring.launch(0, sub)
+        ring.launch_side(0, sub)
+    own = pltpu.make_async_copy(x_ref, big.at[pl.ds(pl.multiple_of(ring.me * rows, rows), rows)], own_sem.at[0])
+    own.start()
+
+    def slot_of(step, mine):
+        return step % 2 * 2 + (0 if mine else 1)
+
+    def fetch(step, mine):
+        slot = slot_of(step, mine)
+        place = pl.ds(ring.block_row(step, mine), rows)
+        return (
+            pltpu.make_async_copy(cin_ref.at[place, :], cbuf.at[slot], cin_sem.at[slot]),
+            pltpu.make_async_copy(rin_ref.at[place, :], rbuf.at[slot], rin_sem.at[slot]),
+        )
+
+    def start_fetch(step, mine):
+        cols, strip = fetch(step, mine)
+        cols.start()
+
+        @pl.when(jnp.logical_not(owner))
+        def _():
+            strip.start()
+
+    for step in range(2):
+        for mine in (True, False):
+            start_fetch(step, mine)
+    ones_r[...] = jnp.ones_like(ones_r)
+    lt[2 * side:, :] = jnp.ones((lt.shape[0] - 2 * side, rows), lt.dtype)
+    acc_ref[...] = jnp.zeros_like(acc_ref)
+    rsum_ref[...] = jnp.zeros_like(rsum_ref)
+    own.wait()
+    tile = min(512, width)
+
+    def work(step, mine):
+        if not mine:
+            ring.beside_arrived(step)
+        ring.side_arrived(step, mine)
+        slot = slot_of(step, mine)
+        place = pl.ds(ring.block_row(step, mine), rows)
+        cols, strip = fetch(step, mine)
+        cols.wait()
+
+        @pl.when(owner)
+        def _():
+            lt[0:side, :] = cbuf[slot, :, pl.ds(ring.feature, side)].T
+            lt[side:2 * side, :] = big[place, pl.ds(ring.feature, side)].T
+
+        @pl.when(jnp.logical_not(owner))
+        def _():
+            strip.wait()
+            lt[0:side, :] = rbuf[slot].T
+            lt[side:2 * side, :] = far[place, :].T
+
+        rsum_ref[...] += jnp.dot(lt[0:2 * side, :], ones_r[...], preferred_element_type=jnp.float32)
+
+        @pl.loop(0, width // tile)
+        def _(i):
+            here = pl.ds(pl.multiple_of(i * tile, tile), tile)
+            acc_ref[:, here] += jnp.dot(
+                lt[...], cbuf[slot, :, here], preferred_element_type=jnp.float32
+            )
+            there = pl.ds(pl.multiple_of(width + i * tile, tile), tile)
+            acc_ref[:, there] += jnp.dot(
+                lt[...], big[place, here], preferred_element_type=jnp.float32
+            )
+
+        if step + 2 < chips:
+            start_fetch(step + 2, mine)
+
+    for step in range(1, chips):
+        for sub in range(SUBS):
+            ring.event(step, sub)
+            ring.launch_side(step, sub)
+            if sub == 0:
+                work(step - 1, True)
+            if sub == SUBS - 1:
+                work(step - 1, False)
+    work(chips - 1, True)
+    work(chips - 1, False)
+    ring.drain()
+
+
+def finish_kernel(all_rows, *refs):
+    rsum_ref, out_ref = refs[4:]
+    side = out_ref.shape[1]
+    for source in range(2):
+        acc_ref, csum_ref = refs[2 * source:2 * source + 2]
+        mean_col = csum_ref[0:1, :] / all_rows
+        for row_source in range(2):
+            part = slice(row_source * side, (row_source + 1) * side)
+            cov = acc_ref[part, :] / all_rows - (rsum_ref[part, :1] / all_rows) * mean_col
+            out_ref[row_source, :, source, :] = cov
+
+
+def joint_cov(hidden_out, rows_in, cols_in, call_id):
+    rows, width = hidden_out.shape
+    all_rows, side = rows_in.shape
+    chips = all_rows // rows // 2
+    dma = pltpu.SemaphoreType.DMA
+    tall = 2 * side + 16
+    acc, rsum = pl.pallas_call(
+        functools.partial(cov_kernel, chips),
+        out_shape=[
+            jax.ShapeDtypeStruct((tall, 2 * width), jnp.float32),
+            jax.ShapeDtypeStruct((2 * side, 128), jnp.float32),
+        ],
+        in_specs=[pl.BlockSpec(memory_space=pltpu.VMEM)]
+        + [pl.BlockSpec(memory_space=pl.ANY)] * 2,
+        out_specs=[pl.BlockSpec(memory_space=pltpu.VMEM)] * 2,
+        scratch_shapes=[
+            pltpu.VMEM((all_rows, width), jnp.bfloat16),
+            pltpu.VMEM((all_rows, side), jnp.bfloat16),
+            pltpu.VMEM((tall, rows), jnp.bfloat16),
+            pltpu.VMEM((4, rows, width), jnp.bfloat16),
+            pltpu.VMEM((4, rows, side), jnp.bfloat16),
+        ]
+        + [dma((chips, SUBS))] * 8
+        + [dma((1,)), dma((4,)), dma((4,))]
+        + [pltpu.VMEM((rows, 128), jnp.bfloat16)],
+        compiler_params=pltpu.CompilerParams(
+            collective_id=call_id, has_side_effects=True, vmem_limit_bytes=VMEM_LIMIT
+        ),
+        cost_estimate=pl.CostEstimate(
+            flops=8 * all_rows * side * width * 4,
+            bytes_accessed=4 * all_rows * (side + width) + 16 * side * width,
+            transcendentals=0,
+        ),
+        name="cov_ring",
+    )(hidden_out, cols_in, rows_in)
+    return finish(acc, rsum, all_rows, side, width)
+
+
+def finish(acc, rsum, all_rows, side, width):
+    tile = min(256, width)
+    strips = width // tile
+    specs = []
+    for source in range(2):
+        specs.append(pl.BlockSpec((2 * side, tile), lambda j, source=source: (0, source * strips + j)))
+        specs.append(
+            pl.BlockSpec((8, tile), lambda j, source=source: (2 * side // 8, source * strips + j))
+        )
+    return pl.pallas_call(
+        functools.partial(finish_kernel, all_rows),
+        out_shape=jax.ShapeDtypeStruct((2, side, 2, width), jnp.float32),
+        grid=(strips,),
+        in_specs=specs + [pl.BlockSpec((2 * side, 128), lambda j: (0, 0))],
+        out_specs=pl.BlockSpec((2, side, 2, tile), lambda j: (0, 0, 0, j)),
+        compiler_params=pltpu.CompilerParams(
+            dimension_semantics=("arbitrary",), vmem_limit_bytes=VMEM_LIMIT
+        ),
+        name="finish",
+    )(acc, acc, acc, acc, rsum)
+
+
+NEG = -1e30
+
+
+def front_kernel(
+    chips, kv_heads, groups, x_ref, gain_ref, cos_ref, sin_ref, kdoc_ref, qdoc_ref,
+    wq_ref, wk_ref, wv_ref, wo_ref, out_ref, cin, far, other, normed, wkv, wq, wo, kv, q_ref,
+    m_ref, l_ref, acc_ref, att, mine_sum, sent, arrived, bias, *sems
+):
+    place = ring_place(chips)
+    hid_sems, side_sems, kv_sems = sems[0:4], sems[4:8], sems[8:12]
+    xsend, xrecv, osend, orecv, own_sem, wkv_sem, wq_sem, wo_sem = sems[12:]
+    rows, width = x_ref.shape
+    side = far.shape[1]
+    hid = Ring(place, cin, x_ref, SUBS, hid_sems, far, side, side_sems)
+    ring = Ring(place, kv, None, SUBS, kv_sems)
+    me, tp = hid.me, hid.tp
+    half = rows // SUBS
+    kv_width = kv_heads * HS
+    scale = HS ** (-0.5) * math.log2(math.e)
+    head_pair = 2 * HS
+    q_tiles = kv_heads * groups // 2
+    out_tile = width // 4
+
+    def swap(sub):
+        part = pl.ds(sub * half, half)
+        return pltpu.make_async_remote_copy(
+            src_ref=x_ref.at[part], dst_ref=other.at[part], send_sem=xsend.at[sub],
+            recv_sem=xrecv.at[sub], device_id={"tp": 1 - tp}, device_id_type=MESH,
+        )
+
+    def fetch_q(t):
+        col = pl.ds(pl.multiple_of(t * head_pair, head_pair), head_pair)
+        return pltpu.make_async_copy(wq_ref.at[:, col], wq.at[t % 4], wq_sem.at[t % 4])
+
+    def fetch_out(side_tp, i):
+        col = pl.ds(pl.multiple_of(side_tp * width + i * out_tile, out_tile), out_tile)
+        return pltpu.make_async_copy(wo_ref.at[:, col], wo.at[i], wo_sem.at[i])
+
+    def out_part(i):
+        return pl.ds(pl.multiple_of(i * out_tile, out_tile), out_tile)
+
+    def give(i):
+        return pltpu.make_async_remote_copy(
+            src_ref=sent.at[:, out_part(i)], dst_ref=arrived.at[:, out_part(i)],
+            send_sem=osend.at[i], recv_sem=orecv.at[i],
+            device_id={"tp": 1 - tp}, device_id_type=MESH,
+        )
+
+    keys = [
+        pltpu.make_async_copy(ref, wkv.at[:, pl.ds(i * kv_width, kv_width)], wkv_sem.at[i])
+        for i, ref in enumerate((wk_ref, wv_ref))
+    ]
+    for copy in keys:
+        copy.start()
+    greet(hid)
+    for sub in range(SUBS):
+        swap(sub).start()
+        hid.launch(0, sub)
+    own = pltpu.make_async_copy(x_ref, cin.at[pl.ds(pl.multiple_of(me * rows, rows), rows)], own_sem.at[0])
+    own.start()
+    for t in range(4):
+        fetch_q(t).start()
+    for i in range(4):
+        fetch_out(1 - tp, i).start()
+
+    @pl.loop(0, kv_heads)
+    def _(g):
+        m_ref[g] = jnp.full(m_ref.shape[1:], NEG, jnp.float32)
+        l_ref[g] = jnp.zeros(l_ref.shape[1:], jnp.float32)
+        acc_ref[g] = jnp.zeros(acc_ref.shape[1:], jnp.float32)
+
+    my_cols = pl.ds(pl.multiple_of(tp * width, width), width)
+    other_cols = pl.ds(pl.multiple_of((1 - tp) * width, width), width)
+
+    def normalise(sub):
+        @pl.loop(0, half // 32)
+        def _(r):
+            part = pl.ds(pl.multiple_of(sub * half + r * 32, 32), 32)
+            near = x_ref[part, :].astype(jnp.float32)
+            away = other[part, :].astype(jnp.float32)
+            total = jnp.sum(near * near, axis=1, keepdims=True) + jnp.sum(away * away, axis=1, keepdims=True)
+            factor = lax.rsqrt(total / (2 * width) + epsilon)
+            normed[part, my_cols] = (near * factor * gain_ref[:, my_cols]).astype(jnp.bfloat16)
+            normed[part, other_cols] = (away * factor * gain_ref[:, other_cols]).astype(jnp.bfloat16)
+
+    def turned(vectors):
+        return vectors * cos_ref[...] + pltpu.roll(vectors, HS // 2, 1) * sin_ref[...]
+
+    hid.event(1, 0)
+    hid.event(1, 1)
+    swap(0).wait_recv()
+    normalise(0)
+    hid.event(2, 0)
+    hid.event(2, 1)
+    swap(1).wait_recv()
+    normalise(1)
+    for copy in keys:
+        copy.wait()
+    my_rows = pl.ds(pl.multiple_of(me * rows, rows), rows)
+
+    @pl.loop(0, kv_width // head_pair)
+    def _(t):
+        col = pl.multiple_of(t * head_pair, head_pair)
+        found = jnp.dot(normed[...], wkv[:, pl.ds(col, head_pair)], preferred_element_type=jnp.float32)
+        for j in range(2):
+            piece = turned(found[:, j * HS:(j + 1) * HS]).astype(jnp.bfloat16)
+            kv[my_rows, pl.ds(pl.multiple_of(col + j * HS, HS), HS)] = piece
+
+    @pl.loop(0, kv_width // head_pair)
+    def _(t):
+        col = pl.ds(pl.multiple_of(kv_width + t * head_pair, head_pair), head_pair)
+        found = jnp.dot(normed[...], wkv[:, col], preferred_element_type=jnp.float32)
+        kv[my_rows, col] = found.astype(jnp.bfloat16)
+
+    for sub in range(SUBS):
+        ring.launch(0, sub)
+    for step in range(3):
+        for sub in range(SUBS):
+            hid.launch_side(step, sub)
+
+    @pl.loop(0, q_tiles)
+    def _(t):
+        fetch_q(t).wait()
+        found = jnp.dot(normed[...], wq[t % 4], preferred_element_type=jnp.float32)
+        for j in range(2):
+            head = t * 2 + j
+            row = pl.multiple_of(head % groups * rows, rows)
+            q_ref[head // groups, pl.ds(row, rows), :] = turned(found[:, j * HS:(j + 1) * HS]).astype(jnp.bfloat16)
+
+        @pl.when(t + 4 < q_tiles)
+        def _():
+            fetch_q(t + 4).start()
+
+        @pl.when(t == q_tiles // 2)
+        def _():
+            ring.event(1, 0)
+
+    ring.event(1, 1)
+
+    def block_attention(row):
+        key_pos = row + lax.broadcasted_iota(jnp.int32, (rows, rows), 1)
+        query_pos = me * rows + lax.broadcasted_iota(jnp.int32, (rows, rows), 0)
+        allowed = (kdoc_ref[:, pl.ds(row, rows)] == qdoc_ref[:, :1]) & (key_pos <= query_pos)
+        bias[...] = jnp.where(allowed, 0.0, NEG)
+
+        @pl.loop(0, kv_heads)
+        def _(g):
+            k = kv[pl.ds(row, rows), pl.ds(pl.multiple_of(g * HS, HS), HS)]
+            v = kv[pl.ds(row, rows), pl.ds(pl.multiple_of(kv_width + g * HS, HS), HS)]
+            for head in range(groups):
+                part = pl.ds(head * rows, rows)
+                s = lax.dot_general(
+                    q_ref[g, part, :], k, (((1,), (1,)), ((), ())), preferred_element_type=jnp.float32
+                ) * scale + bias[...]
+                old = m_ref[g, part, :]
+                top = jnp.maximum(old, jnp.max(s, axis=-1, keepdims=True))
+                fade = jnp.exp2(old - top)
+                weights = [jnp.exp2(s[:, i:i + 128] - top) for i in range(0, rows, 128)]
+                total = l_ref[g, part, :] * fade
+                for piece in weights:
+                    total = total + piece
+                l_ref[g, part, :] = total
+                m_ref[g, part, :] = top
+                acc_ref[g, part, :] = acc_ref[g, part, :] * fade + jnp.dot(
+                    jnp.concatenate(weights, axis=1).astype(jnp.bfloat16), v,
+                    preferred_element_type=jnp.float32,
+                )
+
+    @pl.loop(0, 2 * chips)
+    def _(u):
+        step, which = u // 2, u % 2
+        later = u + 4
+        @pl.when(later < 2 * chips)
+        def _():
+            ring.event(later // 2, later % 2)
+
+        @pl.when(later == 2 * chips - 2)
+        def _():
+            for sub in range(SUBS):
+                hid.event(3, sub)
+                hid.launch_side(3, sub)
+
+        @pl.when(which == 1)
+        def _():
+            ring.beside_arrived(step)
+
+        block = jnp.where(which == 0, ring.block(step, True), ring.block(step, False))
+
+        @pl.when(block <= me)
+        def _():
+            block_attention(pl.multiple_of(block * rows, rows))
+
+    hid.event(4, 0)
+    hid.event(4, 1)
+
+    @pl.loop(0, kv_heads)
+    def _(g):
+        for head in range(groups):
+            part = pl.ds(head * rows, rows)
+            weight_sum = jnp.sum(l_ref[g, part, :], axis=-1, keepdims=True)
+            col = pl.ds(pl.multiple_of((g * groups + head) * HS, HS), HS)
+            att[:, col] = (acc_ref[g, part, :] / weight_sum).astype(jnp.bfloat16)
+
+    @pl.loop(0, 4)
+    def _(i):
+        fetch_out(1 - tp, i).wait()
+        found = jnp.dot(att[...], wo[i], preferred_element_type=jnp.float32)
+        sent[:, out_part(i)] = found.astype(jnp.bfloat16)
+
+        @pl.when(i > 0)
+        def _():
+            give(i - 1).start()
+
+        fetch_out(tp, i).start()
+
+    for sub in range(SUBS):
+        hid.launch_side(4, sub)
+    hid.event(5, 0)
+    give(3).start()
+
+    @pl.loop(0, 4)
+    def _(i):
+        fetch_out(tp, i).wait()
+        mine_sum[:, out_part(i)] = jnp.dot(att[...], wo[i], preferred_element_type=jnp.float32)
+
+    hid.event(5, 1)
+    for sub in range(SUBS):
+        hid.launch_side(5, sub)
+
+    def settle(i):
+        give(i).wait_recv()
+        summed = mine_sum[:, out_part(i)] + arrived[:, out_part(i)].astype(jnp.float32)
+        out_ref[:, out_part(i)] = (x_ref[:, out_part(i)].astype(jnp.float32) + summed).astype(jnp.bfloat16)
+
+    pl.loop(0, 2)(settle)
+    for step in range(6, chips):
+        for sub in range(SUBS):
+            hid.event(step, sub)
+            hid.launch_side(step, sub)
+    pl.loop(2, 4)(settle)
+    own.wait()
+    for step in range(chips):
+        hid.beside_arrived(step)
+        for mine in (True, False):
+            hid.side_arrived(step, mine)
+    hid.drain()
+    ring.drain()
+    for sub in range(SUBS):
+        swap(sub).wait_send()
+    for i in range(4):
+        give(i).wait_send()
+
+
+def front(hidden_in, norm_gain, cosine, sine, doc_ids, query_doc, w_query, w_key, w_value, w_out, call_id):
+    rows, width = hidden_in.shape
+    all_rows = doc_ids.shape[1]
+    chips = all_rows // rows // 2
+    side = width * 2 // (2 * chips)
+    kv_heads = w_key.shape[1] // HS
+    groups = w_query.shape[1] // w_key.shape[1]
+    dma = pltpu.SemaphoreType.DMA
+    bf16, f32 = jnp.bfloat16, jnp.float32
+    stacked = (kv_heads, groups * rows, HS)
+    return pl.pallas_call(
+        functools.partial(front_kernel, chips, kv_heads, groups),
+        out_shape=[
+            jax.ShapeDtypeStruct((rows, width), bf16),
+            jax.ShapeDtypeStruct((all_rows, width), bf16),
+            jax.ShapeDtypeStruct((all_rows, side), bf16),
+        ],
+        in_specs=[pl.BlockSpec(memory_space=pltpu.VMEM)] * 6 + [pl.BlockSpec(memory_space=pl.ANY)] * 4,
+        out_specs=[pl.BlockSpec(memory_space=pltpu.VMEM)] + [pl.BlockSpec(memory_space=pl.ANY)] * 2,
+        scratch_shapes=[
+            pltpu.VMEM((rows, width), bf16),
+            pltpu.VMEM((rows, 2 * width), bf16),
+            pltpu.VMEM((2 * width, 2 * w_key.shape[1]), bf16),
+            pltpu.VMEM((4, 2 * width, 2 * HS), bf16),
+            pltpu.VMEM((4, w_out.shape[0], width // 4), bf16),
+            pltpu.VMEM((all_rows, 2 * w_key.shape[1]), bf16),
+            pltpu.VMEM(stacked, bf16),
+            pltpu.VMEM(stacked, f32),
+            pltpu.VMEM(stacked, f32),
+            pltpu.VMEM(stacked, f32),
+            pltpu.VMEM((rows, w_out.shape[0]), bf16),
+            pltpu.VMEM((rows, width), f32),
+            pltpu.VMEM((rows, width), bf16),
+            pltpu.VMEM((rows, width), bf16),
+            pltpu.VMEM((rows, rows), f32),
+        ]
+        + [dma((chips, SUBS))] * 12
+        + [dma((SUBS,))] * 2
+        + [dma((4,))] * 2
+        + [dma((1,)), dma((2,)), dma((4,)), dma((4,))],
+        compiler_params=pltpu.CompilerParams(
+            collective_id=call_id, has_side_effects=True, vmem_limit_bytes=VMEM_LIMIT
+        ),
+        name="front",
+    )(hidden_in, norm_gain, cosine, sine, doc_ids, query_doc, w_query, w_key, w_value, w_out)
+
+
+def on_pairs(hidden_in, norm_gain, w_query, w_key, w_value, w_out, doc_ids):
+    rows = hidden_in.shape[0]
+    first_row = lax.axis_index("tok") * rows
+    positions = (first_row + jnp.arange(rows, dtype=jnp.int32)) % doc_ids.shape[0]
+    lane = jnp.arange(HS, dtype=jnp.int32)
+    pair = (lane % (HS // 2)).astype(jnp.float32)
+    inv_freq = rope_base ** (-(pair * 2.0) / HS)
+    angles = positions.astype(jnp.float32)[:, None] * inv_freq[None, :]
+    sine = jnp.sin(angles) * jnp.where(lane < HS // 2, -1.0, 1.0)[None, :]
+    query_doc = lax.dynamic_slice_in_dim(doc_ids, first_row, rows, 0)
+    hidden_out, cols_in, rows_in = front(
+        hidden_in, norm_gain[None, :], jnp.cos(angles), sine, doc_ids[None, :],
+        jnp.broadcast_to(query_doc[:, None], (rows, 128)), w_query, w_key, w_value, w_out, 0,
+    )
+    return (hidden_out, joint_cov(hidden_out, rows_in, cols_in, 1))
+
+
 def on_device(hidden_in, norm_gain, w_query, w_key, w_value, w_out, doc_ids):
     tok_rows, col_width = hidden_in.shape
     tok_count = lax.axis_size("tok")
     tp_count = lax.axis_size("tp")
+    if tp_count == 2:
+        return on_pairs(hidden_in, norm_gain, w_query, w_key, w_value, w_out, doc_ids)
     tok_index = lax.axis_index("tok")
     all_rows = tok_rows * tok_count
     full_in = both_sides(hidden_in)
@@ -379,22 +990,11 @@
     bounds = jnp.stack([first_row.astype(jnp.int32), lo[0]])
     attended = attend(queries, kv_rows, jnp.broadcast_to(lo[:, None], (tok_rows, 128)), bounds, kv_heads)
     partial_out = jnp.dot(attended, w_out, preferred_element_type=jnp.float32)
-    if tp_count == 2:
-        first = lax.axis_index("tp") == 0
-        low, high = partial_out[:, :col_width], partial_out[:, col_width:]
-        sent = jnp.where(first, high, low).astype(jnp.bfloat16)
-        arrived = lax.ppermute(sent, "tp", ((0, 1), (1, 0)))
-        summed = jnp.where(first, low, high) + arrived.astype(jnp.float32)
-    else:
-        summed = lax.psum_scatter(partial_out, "tp", scatter_dimension=1, tiled=True)
+    summed = lax.psum_scatter(partial_out, "tp", scatter_dimension=1, tiled=True)
     hidden_out = (hidden_in.astype(jnp.float32) + summed).astype(jnp.bfloat16)
     halves = jnp.stack([hidden_out[:, : col_width // 2], hidden_out[:, col_width // 2 :]])
-    if tp_count == 2:
-        cols_out, arrived_rows = ring_gather(halves, True, 1)
-        rows_out = row_features(cols_out, arrived_rows)
-    else:
-        (cols_out,) = ring_gather(halves, False, 1)
-        rows_out = row_features(cols_out, None)
+    (cols_out,) = ring_gather(halves, False, 1)
+    rows_out = row_features(cols_out, None)
     return (hidden_out, joint_gram(rows_in, rows_out, cols_in, cols_out))
 
 

time: 383 us -> 267 us (0.70)
  starting transfers between devices: 28.6 us -> 0 us
  waiting for transfers between devices: 23 us -> 0 us
  matrix products: 21.8 us -> 0 us
  other arithmetic: 17 us -> 1.26 us
  between operations: 14.3 us -> 0.66 us
  Pallas kernels: 267 us -> 258 us
  local copies, waits for them, and re-layouts: 9.14 us -> 2.49 us
    all_to_all x1 -> x0, starting transfers between devices: 23.4 us -> none  [on_device(): rows_in = lax.all_to_all(full_in, 'tok', 1, 0, tiled=True)]
    ppermute x2 -> x0, waiting for transfers between devices: 22.9 us -> none  [the longest x1 22.9 us: both_sides(): other = lax.ppermute(block, 'tp', ((0, 1), (1, 0)))]
    dot_general x4 -> x0, matrix products: 21.8 us -> none  [the longest x1 8.57 us: on_device(): jnp.dot(normed, w_query, preferred_element_type=jnp.float32)]
    pallas_call x4 -> x3, Pallas kernels: 267 us -> 258 us  [the longest x1 144 us: front(): pl.pallas_call(functools.partial(front_kernel, chips, kv_heads, groups),...]
    select_n x2 -> x1, other arithmetic: 6.22 us -> 0.01 us  [on_pairs(): sine = jnp.sin(angles) * jnp.where(lane < HS // 2, -1.0, 1.0)[None, :]]
    ppermute x2 -> x0, starting transfers between devices: 5.13 us -> none  [the longest x1 3.03 us: both_sides(): other = lax.ppermute(block, 'tp', ((0, 1), (1, 0)))]
    another operation x5 -> x0, other arithmetic: 4.6 us -> none  [the longest x1 1.29 us: on_device(): bounds = jnp.stack([first_row.astype(jnp.int32), lo[0]])]
  transfers between devices with their start and end apart: 5 -> 0, of which waited for: 1 -> 0; matrix products, arithmetic and copies ran while one was open for 11% -> 0% of each run, Pallas kernels for 62% -> 0%
where the time goes in v2:
time: 267 us; the launch traced here: 263 us
  Pallas kernels  258 us (97%)
    pallas_call x1, Pallas kernels, front(): pl.pallas_call(functools.partial(front_kernel, chips, kv_heads, groups),...  144 us
    pallas_call x1, Pallas kernels, joint_cov(): pl.pallas_call(functools.partial(cov_kernel, chips), out_shape=[jax.Shape...  104 us
    pallas_call x1, Pallas kernels, finish(): pl.pallas_call(functools.partial(finish_kernel, all_rows), out_shape=jax....  10.8 us

profile of v2, /device:TPU:0, one launch (start us, length us, event | category | flops | bytes accessed | tf_op | source)
XLA Modules:
  0.0 262.7 jit_solution(15098182200239727483)
XLA Ops:
  0.6 0.8 dynamic_slice.3
  1.4 0.8 broadcast_in_dim.27.qdoc_ref
  2.2 1.2 fusion
  3.4 143.6 %front.1 = (bf16[256,2048]{1,0:T(8,128)(2,1)}, bf16[4096,2048]{1,0:T(8,128)(2,1)}, bf16[4096,256]{1,0:T(8,128)(2,1)}) custom-call(bf16[256,2048]{1,0:T(8,128)(2,1)} %x_ref.1, f32[1,4096]{1,0:T(1,128)} %bitcast.3, f32[256,128]{1,0:T(8,128)} %get-tuple-element.13.cos_ref, f32[256,128]{1,0:T(8,128)} %get-tuple-element.12.sin_ref, s32[1,4096]{1,0:T(1,128)} %bitcast.2, ...), custom_call_target="tpu_custom_call" | custom-call | tf_op jit(solution)/shard_map/front/pallas_call | solution.py:900
  147.0 103.9 %cov_ring.1 = (f32[528,4096]{1,0:T(8,128)}, f32[512,128]{1,0:T(8,128)}) custom-call(bf16[256,2048]{1,0:T(8,128)(2,1)} %get-tuple-element.18.x_ref, bf16[4096,2048]{1,0:T(8,128)(2,1)} %get-tuple-element.8.cin_ref, bf16[4096,256]{1,0:T(8,128)(2,1)} %get-tuple-element.9.rin_ref), custom_call_target="tpu_custom_call" | custom-call | flops 68719476736 | bytes 46137344 | tf_op jit(solution)/shard_map/cov_ring/pallas_call | solution.py:583
  250.9 0.0 copy-start
  250.9 10.8 %finish.1 = f32[2,256,2,2048]{3,2,1,0:T(2,128)} custom-call(f32[528,4096]{1,0:T(8,128)} %get-tuple-element.10.refs_0_.refs_1_.refs_2_.refs_3_, f32[528,4096]{1,0:T(8,128)} %get-tuple-element.10.refs_0_.refs_1_.refs_2_.refs_3_, f32[528,4096]{1,0:T(8,128)} %get-tuple-element.10.refs_0_.refs_1_.refs_2_.refs_3_, ...), custom_call_target="tpu_custom_call" | custom-call | tf_op jit(solution)/shard_map/finish/pallas_call | solution.py:624
  261.7 0.0 copy-done
  261.7 1.0 copy.10
  (2 shorter events, 0.0 us)
Async XLA Ops:
  250.9 10.8 %copy-start = (bf16[256,2048]{1,0:T(8,128)(2,1)S(1)}, bf16[256,2048]{1,0:T(8,128)(2,1)}, u32[]{:S(2)}) copy-start(bf16[256,2048]{1,0:T(8,128)(2,1)} %get-tuple-element.18.x_ref) | copy-start | bytes 3145732

commit v3 on v2

--- a/solution.py
+++ b/solution.py
@@ -343,6 +343,8 @@
 
 
 SUBS = 2
+SIDE_STEPS = 6
+COV_SUBS = 2
 MESH = pl.DeviceIdType.MESH
 
 
@@ -446,13 +448,13 @@
             for sub in range(self.subs):
                 self.side_copy(step, sub, mine).wait_recv()
 
-    def drain(self):
+    def drain(self, side_steps=0):
         for step in range(self.chips):
             for sub in range(self.subs):
                 if step < self.chips - 1:
                     self.ring_copy(step, sub).wait_send()
                 self.beside_copy(step, sub).wait_send()
-                if self.far is not None:
+                if step < side_steps:
                     @pl.when(self.owner)
                     def _():
                         for same in (True, False):
@@ -471,14 +473,15 @@
 
 
 def cov_kernel(chips, x_ref, cin_ref, rin_ref, *refs):
-    acc_ref, rsum_ref, big, far, lt, cbuf, rbuf = refs[:7]
-    sems, side_sems, own_sem, cin_sem, rin_sem, ones_r = refs[7:11], refs[11:15], *refs[15:]
-    ring = Ring(ring_place(chips), big, x_ref, SUBS, sems, far, rin_ref.shape[1], side_sems)
+    acc_ref, rsum_ref, big, far, lt, cbuf, rbuf, late = refs[:8]
+    sems, side_sems = refs[8:12], refs[12:16]
+    own_sem, cin_sem, rin_sem, lsend, lrecv, ones_r = refs[16:]
+    ring = Ring(ring_place(chips), big, x_ref, COV_SUBS, sems, far, rin_ref.shape[1], side_sems)
     rows, width = x_ref.shape
     side = ring.side
     owner = ring.owner
     greet(ring)
-    for sub in range(SUBS):
+    for sub in range(COV_SUBS):
         ring.launch(0, sub)
         ring.launch_side(0, sub)
     own = pltpu.make_async_copy(x_ref, big.at[pl.ds(pl.multiple_of(ring.me * rows, rows), rows)], own_sem.at[0])
@@ -487,25 +490,36 @@
     def slot_of(step, mine):
         return step % 2 * 2 + (0 if mine else 1)
 
-    def fetch(step, mine):
+    def fetch_cols(step, mine):
         slot = slot_of(step, mine)
         place = pl.ds(ring.block_row(step, mine), rows)
-        return (
-            pltpu.make_async_copy(cin_ref.at[place, :], cbuf.at[slot], cin_sem.at[slot]),
-            pltpu.make_async_copy(rin_ref.at[place, :], rbuf.at[slot], rin_sem.at[slot]),
+        return pltpu.make_async_copy(cin_ref.at[place, :], cbuf.at[slot], cin_sem.at[slot])
+
+    def fetch_strip(step, mine):
+        slot = slot_of(step, mine)
+        place = pl.ds(ring.block_row(step, mine), rows)
+        return pltpu.make_async_copy(rin_ref.at[place, :], rbuf.at[slot], rin_sem.at[slot])
+
+    def late_copy(step, same):
+        wanted, target = (ring.feature, ring.me) if same else (ring.partner_feature, ring.partner)
+        slot = (step - SIDE_STEPS) * 2 + (0 if same else 1)
+        return pltpu.make_async_remote_copy(
+            src_ref=cin_ref.at[pl.ds(ring.block_row(step, True), rows), pl.ds(wanted, side)],
+            dst_ref=late.at[slot], send_sem=lsend.at[slot], recv_sem=lrecv.at[slot],
+            device_id={"tok": target, "tp": 1 - ring.tp}, device_id_type=MESH,
         )
 
     def start_fetch(step, mine):
-        cols, strip = fetch(step, mine)
-        cols.start()
-
-        @pl.when(jnp.logical_not(owner))
-        def _():
-            strip.start()
+        fetch_cols(step, mine).start()
+        if step < SIDE_STEPS:
+            @pl.when(jnp.logical_not(owner))
+            def _():
+                fetch_strip(step, mine).start()
 
     for step in range(2):
         for mine in (True, False):
             start_fetch(step, mine)
+
     ones_r[...] = jnp.ones_like(ones_r)
     lt[2 * side:, :] = jnp.ones((lt.shape[0] - 2 * side, rows), lt.dtype)
     acc_ref[...] = jnp.zeros_like(acc_ref)
@@ -519,8 +533,7 @@
         ring.side_arrived(step, mine)
         slot = slot_of(step, mine)
         place = pl.ds(ring.block_row(step, mine), rows)
-        cols, strip = fetch(step, mine)
-        cols.wait()
+        fetch_cols(step, mine).wait()
 
         @pl.when(owner)
         def _():
@@ -529,8 +542,12 @@
 
         @pl.when(jnp.logical_not(owner))
         def _():
-            strip.wait()
-            lt[0:side, :] = rbuf[slot].T
+            if step < SIDE_STEPS:
+                fetch_strip(step, mine).wait()
+                lt[0:side, :] = rbuf[slot].T
+            else:
+                late_copy(step, mine).wait_recv()
+                lt[0:side, :] = late[(step - SIDE_STEPS) * 2 + (0 if mine else 1)].T
             lt[side:2 * side, :] = far[place, :].T
 
         rsum_ref[...] += jnp.dot(lt[0:2 * side, :], ones_r[...], preferred_element_type=jnp.float32)
@@ -550,28 +567,43 @@
             start_fetch(step + 2, mine)
 
     for step in range(1, chips):
-        for sub in range(SUBS):
+        for sub in range(COV_SUBS):
             ring.event(step, sub)
             ring.launch_side(step, sub)
-            if sub == 0:
+            if sub == 0 and 1 <= step <= chips - SIDE_STEPS:
+                @pl.when(owner)
+                def _():
+                    for same in (True, False):
+                        late_copy(SIDE_STEPS + step - 1, same).start()
+            if sub == COV_SUBS // 2 - 1:
                 work(step - 1, True)
-            if sub == SUBS - 1:
+            if sub == COV_SUBS - 1:
                 work(step - 1, False)
     work(chips - 1, True)
     work(chips - 1, False)
-    ring.drain()
-
-
-def finish_kernel(all_rows, *refs):
-    rsum_ref, out_ref = refs[4:]
-    side = out_ref.shape[1]
-    for source in range(2):
-        acc_ref, csum_ref = refs[2 * source:2 * source + 2]
-        mean_col = csum_ref[0:1, :] / all_rows
-        for row_source in range(2):
-            part = slice(row_source * side, (row_source + 1) * side)
-            cov = acc_ref[part, :] / all_rows - (rsum_ref[part, :1] / all_rows) * mean_col
-            out_ref[row_source, :, source, :] = cov
+    ring.drain(chips)
+
+    @pl.when(owner)
+    def _():
+        for step in range(SIDE_STEPS, chips):
+            for same in (True, False):
+                late_copy(step, same).wait_send()
+
+
+def finish_kernel(all_rows, width, upper_ref, lower_ref, csum_ref, rtop_ref, rlow_ref, x_ref, out_ref, y_ref):
+    tall = upper_ref.shape[0]
+    groups = 2 * width // 128
+    part_of = 1.0 / all_rows
+    y_ref[...] = x_ref[...]
+    for row_source, (acc_ref, rsum_ref) in enumerate(((upper_ref, rtop_ref), (lower_ref, rlow_ref))):
+        mean_row = rsum_ref[...] * part_of
+        for source in range(2):
+            for j in range(width // 128):
+                part = slice(source * width + j * 128, source * width + (j + 1) * 128)
+                mean_col = csum_ref[0:1, part] * part_of
+                out_ref[row_source, pl.ds(2 * j + source, tall, stride=groups), :] = (
+                    acc_ref[:, part] * part_of - mean_row * mean_col
+                )
 
 
 def joint_cov(hidden_out, rows_in, cols_in, call_id):
@@ -595,12 +627,14 @@
             pltpu.VMEM((tall, rows), jnp.bfloat16),
             pltpu.VMEM((4, rows, width), jnp.bfloat16),
             pltpu.VMEM((4, rows, side), jnp.bfloat16),
+            pltpu.VMEM((2 * (chips - SIDE_STEPS), rows, side), jnp.bfloat16),
         ]
-        + [dma((chips, SUBS))] * 8
+        + [dma((chips, COV_SUBS))] * 8
         + [dma((1,)), dma((4,)), dma((4,))]
+        + [dma((2 * (chips - SIDE_STEPS),))] * 2
         + [pltpu.VMEM((rows, 128), jnp.bfloat16)],
         compiler_params=pltpu.CompilerParams(
-            collective_id=call_id, has_side_effects=True, vmem_limit_bytes=VMEM_LIMIT
+            collective_id=call_id, has_side_effects=True, vmem_limit_bytes=38 * 1024 * 1024
         ),
         cost_estimate=pl.CostEstimate(
             flops=8 * all_rows * side * width * 4,
@@ -609,38 +643,51 @@
         ),
         name="cov_ring",
     )(hidden_out, cols_in, rows_in)
-    return finish(acc, rsum, all_rows, side, width)
-
-
-def finish(acc, rsum, all_rows, side, width):
-    tile = min(256, width)
-    strips = width // tile
-    specs = []
-    for source in range(2):
-        specs.append(pl.BlockSpec((2 * side, tile), lambda j, source=source: (0, source * strips + j)))
-        specs.append(
-            pl.BlockSpec((8, tile), lambda j, source=source: (2 * side // 8, source * strips + j))
-        )
-    return pl.pallas_call(
-        functools.partial(finish_kernel, all_rows),
-        out_shape=jax.ShapeDtypeStruct((2, side, 2, width), jnp.float32),
+    cov, settled = finish(acc, rsum, hidden_out, side)
+    return settled, cov
+
+
+def finish(acc, rsum, hidden_out, side):
+    rows, width = hidden_out.shape
+    all_rows = rows * lax.axis_size("tok")
+    strips = 8
+    tall = side // strips
+    groups = 2 * width // 128
+    cov, settled = pl.pallas_call(
+        functools.partial(finish_kernel, all_rows, width),
+        out_shape=[
+            jax.ShapeDtypeStruct((2, side * groups, 128), jnp.float32),
+            jax.ShapeDtypeStruct(hidden_out.shape, hidden_out.dtype),
+        ],
         grid=(strips,),
-        in_specs=specs + [pl.BlockSpec((2 * side, 128), lambda j: (0, 0))],
-        out_specs=pl.BlockSpec((2, side, 2, tile), lambda j: (0, 0, 0, j)),
+        in_specs=[
+            pl.BlockSpec((tall, 2 * width), lambda i: (i, 0)),
+            pl.BlockSpec((tall, 2 * width), lambda i: (strips + i, 0)),
+            pl.BlockSpec((8, 2 * width), lambda i: (2 * side // 8, 0)),
+            pl.BlockSpec((tall, 128), lambda i: (i, 0)),
+            pl.BlockSpec((tall, 128), lambda i: (strips + i, 0)),
+            pl.BlockSpec((rows // strips, width), lambda i: (i, 0)),
+        ],
+        out_specs=[
+            pl.BlockSpec((2, tall * groups, 128), lambda i: (0, i, 0)),
+            pl.BlockSpec((rows // strips, width), lambda i: (i, 0)),
+        ],
         compiler_params=pltpu.CompilerParams(
-            dimension_semantics=("arbitrary",), vmem_limit_bytes=VMEM_LIMIT
+            dimension_semantics=("arbitrary",), vmem_limit_bytes=8 * 1024 * 1024
         ),
         name="finish",
-    )(acc, acc, acc, acc, rsum)
+    )(acc, acc, acc, rsum, rsum, hidden_out)
+    cov = cov.reshape(2, side, width // 128, 2, 128).transpose(0, 1, 3, 2, 4)
+    return cov.reshape(2, side, 2, width), settled
 
 
 NEG = -1e30
 
 
 def front_kernel(
-    chips, kv_heads, groups, x_ref, gain_ref, cos_ref, sin_ref, kdoc_ref, qdoc_ref,
+    chips, kv_heads, groups, x_ref, gain_ref, cos_ref, sin_ref, kdoc_ref,
     wq_ref, wk_ref, wv_ref, wo_ref, out_ref, cin, far, other, normed, wkv, wq, wo, kv, q_ref,
-    m_ref, l_ref, acc_ref, att, mine_sum, sent, arrived, bias, *sems
+    m_ref, l_ref, acc_ref, att, mine_sum, sent, arrived, bias, qdoc_ref, *sems
 ):
     place = ring_place(chips)
     hid_sems, side_sems, kv_sems = sems[0:4], sems[4:8], sems[8:12]
@@ -705,6 +752,8 @@
         l_ref[g] = jnp.zeros(l_ref.shape[1:], jnp.float32)
         acc_ref[g] = jnp.zeros(acc_ref.shape[1:], jnp.float32)
 
+    my_doc = kdoc_ref[:, pl.ds(pl.multiple_of(me * rows, rows), rows)]
+    qdoc_ref[...] = jnp.broadcast_to(my_doc, (128, rows)).T
     my_cols = pl.ds(pl.multiple_of(tp * width, width), width)
     other_cols = pl.ds(pl.multiple_of((1 - tp) * width, width), width)
 
@@ -732,21 +781,22 @@
     normalise(1)
     for copy in keys:
         copy.wait()
-    my_rows = pl.ds(pl.multiple_of(me * rows, rows), rows)
+    my_base = pl.multiple_of(me * 2 * kv_width, 2 * kv_width)
 
     @pl.loop(0, kv_width // head_pair)
     def _(t):
         col = pl.multiple_of(t * head_pair, head_pair)
         found = jnp.dot(normed[...], wkv[:, pl.ds(col, head_pair)], preferred_element_type=jnp.float32)
         for j in range(2):
-            piece = turned(found[:, j * HS:(j + 1) * HS]).astype(jnp.bfloat16)
-            kv[my_rows, pl.ds(pl.multiple_of(col + j * HS, HS), HS)] = piece
+            piece = turned(found[:, j * HS:(j + 1) * HS])
+            kv[pl.ds(pl.multiple_of(my_base + col + j * HS, HS), HS), :] = piece.T.astype(jnp.bfloat16)
+
 
     @pl.loop(0, kv_width // head_pair)
     def _(t):
-        col = pl.ds(pl.multiple_of(kv_width + t * head_pair, head_pair), head_pair)
-        found = jnp.dot(normed[...], wkv[:, col], preferred_element_type=jnp.float32)
-        kv[my_rows, col] = found.astype(jnp.bfloat16)
+        col = pl.multiple_of(kv_width + t * head_pair, head_pair)
+        found = jnp.dot(normed[...], wkv[:, pl.ds(col, head_pair)], preferred_element_type=jnp.float32)
+        kv[pl.ds(pl.multiple_of(my_base + col, head_pair), rows), :] = found.astype(jnp.bfloat16)
 
     for sub in range(SUBS):
         ring.launch(0, sub)
@@ -773,61 +823,75 @@
 
     ring.event(1, 1)
 
-    def block_attention(row):
-        key_pos = row + lax.broadcasted_iota(jnp.int32, (rows, rows), 1)
-        query_pos = me * rows + lax.broadcasted_iota(jnp.int32, (rows, rows), 0)
-        allowed = (kdoc_ref[:, pl.ds(row, rows)] == qdoc_ref[:, :1]) & (key_pos <= query_pos)
-        bias[...] = jnp.where(allowed, 0.0, NEG)
-
-        @pl.loop(0, kv_heads)
+    def make_bias(blocks):
+        for i, block in enumerate(blocks):
+            row = pl.multiple_of(block * rows, rows)
+            key_pos = row + lax.broadcasted_iota(jnp.int32, (rows, rows), 1)
+            query_pos = me * rows + lax.broadcasted_iota(jnp.int32, (rows, rows), 0)
+            allowed = (kdoc_ref[:, pl.ds(row, rows)] == qdoc_ref[:, :1]) & (key_pos <= query_pos)
+            bias[:, i * rows:(i + 1) * rows] = jnp.where(allowed, 0.0, NEG)
+
+    def pair_attention(blocks, heads):
+        @pl.loop(*heads)
         def _(g):
-            k = kv[pl.ds(row, rows), pl.ds(pl.multiple_of(g * HS, HS), HS)]
-            v = kv[pl.ds(row, rows), pl.ds(pl.multiple_of(kv_width + g * HS, HS), HS)]
+            k_row, v_row = g * HS, kv_width + g // 2 * rows
+            v_col = pl.ds(pl.multiple_of(g % 2 * HS, HS), HS)
+            k = jnp.concatenate(
+                [kv[pl.ds(pl.multiple_of(b * 2 * kv_width + k_row, HS), HS), :] for b in blocks], axis=1
+            )
+            v = jnp.concatenate(
+                [kv[pl.ds(pl.multiple_of(b * 2 * kv_width + v_row, rows), rows), v_col] for b in blocks],
+                axis=0,
+            )
             for head in range(groups):
                 part = pl.ds(head * rows, rows)
-                s = lax.dot_general(
-                    q_ref[g, part, :], k, (((1,), (1,)), ((), ())), preferred_element_type=jnp.float32
-                ) * scale + bias[...]
+                s = jnp.dot(q_ref[g, part, :], k, preferred_element_type=jnp.float32) * scale + bias[...]
                 old = m_ref[g, part, :]
-                top = jnp.maximum(old, jnp.max(s, axis=-1, keepdims=True))
+                pieces = [s[:, i:i + 128] for i in range(0, 2 * rows, 128)]
+                peak = functools.reduce(jnp.maximum, pieces)
+                top = jnp.maximum(old, jnp.max(peak, axis=-1, keepdims=True))
                 fade = jnp.exp2(old - top)
-                weights = [jnp.exp2(s[:, i:i + 128] - top) for i in range(0, rows, 128)]
-                total = l_ref[g, part, :] * fade
-                for piece in weights:
-                    total = total + piece
-                l_ref[g, part, :] = total
+                weights = [jnp.exp2(piece - top) for piece in pieces]
+                l_ref[g, part, :] = l_ref[g, part, :] * fade + functools.reduce(jnp.add, weights)
                 m_ref[g, part, :] = top
                 acc_ref[g, part, :] = acc_ref[g, part, :] * fade + jnp.dot(
                     jnp.concatenate(weights, axis=1).astype(jnp.bfloat16), v,
                     preferred_element_type=jnp.float32,
                 )
 
-    @pl.loop(0, 2 * chips)
-    def _(u):
-        step, which = u // 2, u % 2
-        later = u + 4
-        @pl.when(later < 2 * chips)
-        def _():
-            ring.event(later // 2, later % 2)
-
-        @pl.when(later == 2 * chips - 2)
-        def _():
-            for sub in range(SUBS):
-                hid.event(3, sub)
-                hid.launch_side(3, sub)
-
-        @pl.when(which == 1)
+    @pl.loop(0, chips * SUBS)
+    def _(turn):
+        step, sub = turn // SUBS, turn % SUBS
+
+        @pl.when(step + 2 < chips)
+        def _():
+            ring.event(step + 2, sub)
+
+
+        @pl.when(step + 2 == chips - 1)
+        def _():
+            hid.event(3, sub)
+            hid.launch_side(3, sub)
+
+        @pl.when(step + 2 == chips + 1)
+        def _():
+            hid.event(4, sub)
+            hid.launch_side(4, sub)
+
+        blocks = (ring.block(step, True), ring.block(step, False))
+        needed = (blocks[0] <= me) | (blocks[1] <= me)
+
+        @pl.when(sub == 0)
         def _():
             ring.beside_arrived(step)
 
-        block = jnp.where(which == 0, ring.block(step, True), ring.block(step, False))
-
-        @pl.when(block <= me)
-        def _():
-            block_attention(pl.multiple_of(block * rows, rows))
-
-    hid.event(4, 0)
-    hid.event(4, 1)
+        @pl.when((sub == 0) & needed)
+        def _():
+            make_bias(blocks)
+
+        @pl.when(needed)
+        def _():
+            pair_attention(blocks, (sub * (kv_heads // SUBS), (sub + 1) * (kv_heads // SUBS)))
 
     @pl.loop(0, kv_heads)
     def _(g):
@@ -849,37 +913,34 @@
 
         fetch_out(tp, i).start()
 
-    for sub in range(SUBS):
-        hid.launch_side(4, sub)
-    hid.event(5, 0)
     give(3).start()
+    for i in range(2):
+        hid.event(5, i)
+        hid.launch_side(5, i)
+    hid.event(6, 0)
 
     @pl.loop(0, 4)
     def _(i):
         fetch_out(tp, i).wait()
         mine_sum[:, out_part(i)] = jnp.dot(att[...], wo[i], preferred_element_type=jnp.float32)
 
-    hid.event(5, 1)
-    for sub in range(SUBS):
-        hid.launch_side(5, sub)
+    hid.event(6, 1)
 
     def settle(i):
         give(i).wait_recv()
         summed = mine_sum[:, out_part(i)] + arrived[:, out_part(i)].astype(jnp.float32)
         out_ref[:, out_part(i)] = (x_ref[:, out_part(i)].astype(jnp.float32) + summed).astype(jnp.bfloat16)
 
-    pl.loop(0, 2)(settle)
-    for step in range(6, chips):
-        for sub in range(SUBS):
-            hid.event(step, sub)
-            hid.launch_side(step, sub)
-    pl.loop(2, 4)(settle)
+    pl.loop(0, 4)(settle)
+    for sub in range(SUBS):
+        hid.event(7, sub)
     own.wait()
     for step in range(chips):
         hid.beside_arrived(step)
-        for mine in (True, False):
-            hid.side_arrived(step, mine)
-    hid.drain()
+        if step < SIDE_STEPS:
+            for mine in (True, False):
+                hid.side_arrived(step, mine)
+    hid.drain(SIDE_STEPS)
     ring.drain()
     for sub in range(SUBS):
         swap(sub).wait_send()
@@ -887,7 +948,7 @@
         give(i).wait_send()
 
 
-def front(hidden_in, norm_gain, cosine, sine, doc_ids, query_doc, w_query, w_key, w_value, w_out, call_id):
+def front(hidden_in, norm_gain, cosine, sine, doc_ids, w_query, w_key, w_value, w_out, call_id):
     rows, width = hidden_in.shape
     all_rows = doc_ids.shape[1]
     chips = all_rows // rows // 2
@@ -904,7 +965,7 @@
             jax.ShapeDtypeStruct((all_rows, width), bf16),
             jax.ShapeDtypeStruct((all_rows, side), bf16),
         ],
-        in_specs=[pl.BlockSpec(memory_space=pltpu.VMEM)] * 6 + [pl.BlockSpec(memory_space=pl.ANY)] * 4,
+        in_specs=[pl.BlockSpec(memory_space=pltpu.VMEM)] * 5 + [pl.BlockSpec(memory_space=pl.ANY)] * 4,
         out_specs=[pl.BlockSpec(memory_space=pltpu.VMEM)] + [pl.BlockSpec(memory_space=pl.ANY)] * 2,
         scratch_shapes=[
             pltpu.VMEM((rows, width), bf16),
@@ -912,7 +973,7 @@
             pltpu.VMEM((2 * width, 2 * w_key.shape[1]), bf16),
             pltpu.VMEM((4, 2 * width, 2 * HS), bf16),
             pltpu.VMEM((4, w_out.shape[0], width // 4), bf16),
-            pltpu.VMEM((all_rows, 2 * w_key.shape[1]), bf16),
+            pltpu.VMEM((all_rows // rows * 2 * w_key.shape[1], rows), bf16),
             pltpu.VMEM(stacked, bf16),
             pltpu.VMEM(stacked, f32),
             pltpu.VMEM(stacked, f32),
@@ -921,7 +982,8 @@
             pltpu.VMEM((rows, width), f32),
             pltpu.VMEM((rows, width), bf16),
             pltpu.VMEM((rows, width), bf16),
-            pltpu.VMEM((rows, rows), f32),
+            pltpu.VMEM((rows, 2 * rows), f32),
+            pltpu.VMEM((rows, 128), jnp.int32),
         ]
         + [dma((chips, SUBS))] * 12
         + [dma((SUBS,))] * 2
@@ -931,7 +993,7 @@
             collective_id=call_id, has_side_effects=True, vmem_limit_bytes=VMEM_LIMIT
         ),
         name="front",
-    )(hidden_in, norm_gain, cosine, sine, doc_ids, query_doc, w_query, w_key, w_value, w_out)
+    )(hidden_in, norm_gain, cosine, sine, doc_ids, w_query, w_key, w_value, w_out)
 
 
 def on_pairs(hidden_in, norm_gain, w_query, w_key, w_value, w_out, doc_ids):
@@ -943,19 +1005,18 @@
     inv_freq = rope_base ** (-(pair * 2.0) / HS)
     angles = positions.astype(jnp.float32)[:, None] * inv_freq[None, :]
     sine = jnp.sin(angles) * jnp.where(lane < HS // 2, -1.0, 1.0)[None, :]
-    query_doc = lax.dynamic_slice_in_dim(doc_ids, first_row, rows, 0)
     hidden_out, cols_in, rows_in = front(
         hidden_in, norm_gain[None, :], jnp.cos(angles), sine, doc_ids[None, :],
-        jnp.broadcast_to(query_doc[:, None], (rows, 128)), w_query, w_key, w_value, w_out, 0,
+        w_query, w_key, w_value, w_out, 0,
     )
-    return (hidden_out, joint_cov(hidden_out, rows_in, cols_in, 1))
+    return joint_cov(hidden_out, rows_in, cols_in, 1)
 
 
 def on_device(hidden_in, norm_gain, w_query, w_key, w_value, w_out, doc_ids):
     tok_rows, col_width = hidden_in.shape
     tok_count = lax.axis_size("tok")
     tp_count = lax.axis_size("tp")
-    if tp_count == 2:
+    if tp_count == 2 and tok_rows == 2 * HS and w_key.shape[1] % (2 * HS) == 0:
         return on_pairs(hidden_in, norm_gain, w_query, w_key, w_value, w_out, doc_ids)
     tok_index = lax.axis_index("tok")
     all_rows = tok_rows * tok_count

time: 267 us -> 238 us (0.89); the launches traced: 263 us -> 238 us
  Pallas kernels: 258 us -> 233 us
    pallas_call x1, Pallas kernels: 104 us -> 91.5 us  [joint_cov(): pl.pallas_call(functools.partial(cov_kernel, chips), out_shape=[jax.Shape...]
    pallas_call x1, Pallas kernels: 144 us -> 132 us  [front(): pl.pallas_call(functools.partial(front_kernel, chips, kv_heads, groups),...]
where the time goes in v3:
time: 238 us
  Pallas kernels  233 us (98%)
  local copies, waits for them, and re-layouts  2.81 us (1%)
    pallas_call x1, Pallas kernels, front(): pl.pallas_call(functools.partial(front_kernel, chips, kv_heads, groups),...  132 us
    pallas_call x1, Pallas kernels, joint_cov(): pl.pallas_call(functools.partial(cov_kernel, chips), out_shape=[jax.Shape...  91.5 us
    pallas_call x1, Pallas kernels, finish(): pl.pallas_call(functools.partial(finish_kernel, all_rows, width), out_sha...  9.49 us

profile of v3, /device:TPU:0, one launch (start us, length us, event | category | flops | bytes accessed | tf_op | source)
XLA Modules:
  0.0 238.1 jit_solution(7099126302280827081)
XLA Ops:
  0.7 1.2 fusion
  1.9 132.4 %front.1 = (bf16[256,2048]{1,0:T(8,128)(2,1)}, bf16[4096,2048]{1,0:T(8,128)(2,1)}, bf16[4096,256]{1,0:T(8,128)(2,1)}) custom-call(bf16[256,2048]{1,0:T(8,128)(2,1)} %x_ref.1, f32[1,4096]{1,0:T(1,128)} %bitcast.7, f32[256,128]{1,0:T(8,128)} %get-tuple-element.17.cos_ref, f32[256,128]{1,0:T(8,128)} %get-tuple-element.16.sin_ref, s32[1,4096]{1,0:T(1,128)} %bitcast.8, ...), custom_call_target="tpu_custom_call" | custom-call | tf_op jit(solution)/shard_map/front/pallas_call | solution.py:961
  134.3 0.0 copy-start
  134.3 1.2 copy-done
  135.5 0.0 copy-start.1
  135.5 1.6 copy-done.1
  137.1 91.5 %cov_ring.1 = (f32[528,4096]{1,0:T(8,128)S(1)}, f32[512,128]{1,0:T(8,128)S(1)}) custom-call(bf16[256,2048]{1,0:T(8,128)(2,1)S(1)} %copy-done, bf16[4096,2048]{1,0:T(8,128)(2,1)} %get-tuple-element.10.cin_ref, bf16[4096,256]{1,0:T(8,128)(2,1)S(1)} %copy-done.1), custom_call_target="tpu_custom_call" | custom-call | flops 68719476736 | bytes 46137344 | tf_op jit(solution)/shard_map/cov_ring/pallas_call | solution.py:615
  228.6 9.5 %finish.1 = (f32[2,8192,128]{2,1,0:T(8,128)}, bf16[256,2048]{1,0:T(8,128)(2,1)}) custom-call(f32[528,4096]{1,0:T(8,128)S(1)} %get-tuple-element.12.upper_ref.lower_ref.csum_ref, f32[528,4096]{1,0:T(8,128)S(1)} %get-tuple-element.12.upper_ref.lower_ref.csum_ref, f32[528,4096]{1,0:T(8,128)S(1)} %get-tuple-element.12.upper_ref.lower_ref.csum_ref, ...), custom_call_target="tpu_custom_call" | custom-call | tf_op jit(solution)/shard_map/finish/pallas_call | solution.py:656
  (2 shorter events, 0.0 us)
Async XLA Ops:
  134.3 1.2 copy-start
  135.5 1.6 copy-start.1

commit v4 on v3

--- a/solution.py
+++ b/solution.py
@@ -577,7 +577,7 @@
                         late_copy(SIDE_STEPS + step - 1, same).start()
             if sub == COV_SUBS // 2 - 1:
                 work(step - 1, True)
-            if sub == COV_SUBS - 1:
+            if sub == (COV_SUBS // 2 if step == chips - 1 else COV_SUBS) - 1:
                 work(step - 1, False)
     work(chips - 1, True)
     work(chips - 1, False)
@@ -590,25 +590,28 @@
                 late_copy(step, same).wait_send()
 
 
-def finish_kernel(all_rows, width, upper_ref, lower_ref, csum_ref, rtop_ref, rlow_ref, x_ref, out_ref, y_ref):
-    tall = upper_ref.shape[0]
+def finish_kernel(all_rows, strips, acc_ref, rsum_ref, x_ref, out_ref, y_ref):
+    width = acc_ref.shape[1] // 2
+    side = rsum_ref.shape[0] // 2
+    tall = side // strips
     groups = 2 * width // 128
     part_of = 1.0 / all_rows
     y_ref[...] = x_ref[...]
-    for row_source, (acc_ref, rsum_ref) in enumerate(((upper_ref, rtop_ref), (lower_ref, rlow_ref))):
-        mean_row = rsum_ref[...] * part_of
+    for row_source in range(2):
+        place = pl.ds(pl.multiple_of(row_source * side + pl.program_id(0) * tall, tall), tall)
+        mean_row = rsum_ref[place, :] * part_of
         for source in range(2):
             for j in range(width // 128):
                 part = slice(source * width + j * 128, source * width + (j + 1) * 128)
-                mean_col = csum_ref[0:1, part] * part_of
+                mean_col = acc_ref[2 * side:2 * side + 1, part] * part_of
                 out_ref[row_source, pl.ds(2 * j + source, tall, stride=groups), :] = (
-                    acc_ref[:, part] * part_of - mean_row * mean_col
+                    acc_ref[place, part] * part_of - mean_row * mean_col
                 )
 
 
 def joint_cov(hidden_out, rows_in, cols_in, call_id):
     rows, width = hidden_out.shape
-    all_rows, side = rows_in.shape
+    all_rows, side = cols_in.shape[0], rows_in.shape[1]
     chips = all_rows // rows // 2
     dma = pltpu.SemaphoreType.DMA
     tall = 2 * side + 16
@@ -654,18 +657,15 @@
     tall = side // strips
     groups = 2 * width // 128
     cov, settled = pl.pallas_call(
-        functools.partial(finish_kernel, all_rows, width),
+        functools.partial(finish_kernel, all_rows, strips),
         out_shape=[
             jax.ShapeDtypeStruct((2, side * groups, 128), jnp.float32),
             jax.ShapeDtypeStruct(hidden_out.shape, hidden_out.dtype),
         ],
         grid=(strips,),
         in_specs=[
-            pl.BlockSpec((tall, 2 * width), lambda i: (i, 0)),
-            pl.BlockSpec((tall, 2 * width), lambda i: (strips + i, 0)),
-            pl.BlockSpec((8, 2 * width), lambda i: (2 * side // 8, 0)),
-            pl.BlockSpec((tall, 128), lambda i: (i, 0)),
-            pl.BlockSpec((tall, 128), lambda i: (strips + i, 0)),
+            pl.BlockSpec(memory_space=pltpu.VMEM),
+            pl.BlockSpec(memory_space=pltpu.VMEM),
             pl.BlockSpec((rows // strips, width), lambda i: (i, 0)),
         ],
         out_specs=[
@@ -676,7 +676,7 @@
             dimension_semantics=("arbitrary",), vmem_limit_bytes=8 * 1024 * 1024
         ),
         name="finish",
-    )(acc, acc, acc, rsum, rsum, hidden_out)
+    )(acc, rsum, hidden_out)
     cov = cov.reshape(2, side, width // 128, 2, 128).transpose(0, 1, 3, 2, 4)
     return cov.reshape(2, side, 2, width), settled
 
@@ -798,8 +798,11 @@
         found = jnp.dot(normed[...], wkv[:, pl.ds(col, head_pair)], preferred_element_type=jnp.float32)
         kv[pl.ds(pl.multiple_of(my_base + col, head_pair), rows), :] = found.astype(jnp.bfloat16)
 
-    for sub in range(SUBS):
-        ring.launch(0, sub)
+        @pl.when(t == 0)
+        def _():
+            ring.launch(0, 0)
+
+    ring.launch(0, 1)
     for step in range(3):
         for sub in range(SUBS):
             hid.launch_side(step, sub)
@@ -868,10 +871,11 @@
             ring.event(step + 2, sub)
 
 
-        @pl.when(step + 2 == chips - 1)
-        def _():
-            hid.event(3, sub)
-            hid.launch_side(3, sub)
+        @pl.when((step + 2 == chips - 2) & (sub == 1))
+        def _():
+            for part in range(SUBS):
+                hid.event(3, part)
+                hid.launch_side(3, part)
 
         @pl.when(step + 2 == chips + 1)
         def _():
@@ -963,7 +967,7 @@
         out_shape=[
             jax.ShapeDtypeStruct((rows, width), bf16),
             jax.ShapeDtypeStruct((all_rows, width), bf16),
-            jax.ShapeDtypeStruct((all_rows, side), bf16),
+            jax.ShapeDtypeStruct((8 * all_rows, side), bf16),
         ],
         in_specs=[pl.BlockSpec(memory_space=pltpu.VMEM)] * 5 + [pl.BlockSpec(memory_space=pl.ANY)] * 4,
         out_specs=[pl.BlockSpec(memory_space=pltpu.VMEM)] + [pl.BlockSpec(memory_space=pl.ANY)] * 2,
@@ -990,7 +994,7 @@
         + [dma((4,))] * 2
         + [dma((1,)), dma((2,)), dma((4,)), dma((4,))],
         compiler_params=pltpu.CompilerParams(
-            collective_id=call_id, has_side_effects=True, vmem_limit_bytes=VMEM_LIMIT
+            collective_id=call_id, has_side_effects=True, vmem_limit_bytes=52 * 1024 * 1024
         ),
         name="front",
     )(hidden_in, norm_gain, cosine, sine, doc_ids, w_query, w_key, w_value, w_out)

time: 238 us -> 234 us (0.983)
  Pallas kernels: 233 us -> 230 us
where the time goes in v4:
time: 234 us; the launch traced here: 233 us
  Pallas kernels  230 us (98%)
    pallas_call x1, Pallas kernels, front(): pl.pallas_call(functools.partial(front_kernel, chips, kv_heads, groups),...  131 us
    pallas_call x1, Pallas kernels, joint_cov(): pl.pallas_call(functools.partial(cov_kernel, chips), out_shape=[jax.Shape...  89.7 us
    pallas_call x1, Pallas kernels, finish(): pl.pallas_call(functools.partial(finish_kernel, all_rows, strips), out_sh...  9.42 us

profile of v4, /device:TPU:0, one launch (start us, length us, event | category | flops | bytes accessed | tf_op | source)
XLA Modules:
  0.0 232.8 jit_solution(17378959506509461792)
XLA Ops:
  0.7 0.5 fusion
  1.2 0.0 copy-start
  1.2 0.7 copy-done
  1.9 0.0 copy-start.1
  1.9 0.7 copy-done.1
  2.6 131.0 %front.1 = (bf16[256,2048]{1,0:T(8,128)(2,1)S(1)}, bf16[4096,2048]{1,0:T(8,128)(2,1)}, bf16[32768,256]{1,0:T(8,128)(2,1)}) custom-call(bf16[256,2048]{1,0:T(8,128)(2,1)} %x_ref.1, f32[1,4096]{1,0:T(1,128)S(1)} %bitcast.7, f32[256,128]{1,0:T(8,128)S(1)} %get-tuple-element.17.cos_ref, f32[256,128]{1,0:T(8,128)S(1)} %get-tuple-element.16.sin_ref, ...), custom_call_target="tpu_custom_call" | custom-call | tf_op jit(solution)/shard_map/front/pallas_call | solution.py:965
  133.7 89.7 %cov_ring.1 = (f32[528,4096]{1,0:T(8,128)S(1)}, f32[512,128]{1,0:T(8,128)S(1)}) custom-call(bf16[256,2048]{1,0:T(8,128)(2,1)S(1)} %get-tuple-element.9.x_ref, bf16[4096,2048]{1,0:T(8,128)(2,1)} %get-tuple-element.10.cin_ref, bf16[32768,256]{1,0:T(8,128)(2,1)} %get-tuple-element.11.rin_ref), custom_call_target="tpu_custom_call" | custom-call | flops 68719476736 | bytes 46137344 | tf_op jit(solution)/shard_map/cov_ring/pallas_call | solution.py:618
  223.4 9.4 %finish.1 = (f32[2,8192,128]{2,1,0:T(8,128)}, bf16[256,2048]{1,0:T(8,128)(2,1)}) custom-call(f32[528,4096]{1,0:T(8,128)S(1)} %get-tuple-element.12.acc_ref, f32[512,128]{1,0:T(8,128)S(1)} %get-tuple-element.13.rsum_ref, bf16[256,2048]{1,0:T(8,128)(2,1)S(1)} %get-tuple-element.9.x_ref), custom_call_target="tpu_custom_call" | custom-call | tf_op jit(solution)/shard_map/finish/pallas_call | solution.py:659
  (2 shorter events, 0.0 us)
Async XLA Ops:
  1.2 0.7 copy-start
  1.9 0.7 copy-start.1

commit v5 on v4

--- a/solution.py
+++ b/solution.py
@@ -598,15 +598,18 @@
     part_of = 1.0 / all_rows
     y_ref[...] = x_ref[...]
     for row_source in range(2):
-        place = pl.ds(pl.multiple_of(row_source * side + pl.program_id(0) * tall, tall), tall)
-        mean_row = rsum_ref[place, :] * part_of
-        for source in range(2):
+        for first in range(0, tall, 8):
+            row = row_source * side + pl.program_id(0) * tall + first
+            place = pl.ds(pl.multiple_of(row, 8), 8)
+            mean_row = rsum_ref[place, :] * part_of
+            pieces = []
             for j in range(width // 128):
-                part = slice(source * width + j * 128, source * width + (j + 1) * 128)
-                mean_col = acc_ref[2 * side:2 * side + 1, part] * part_of
-                out_ref[row_source, pl.ds(2 * j + source, tall, stride=groups), :] = (
-                    acc_ref[place, part] * part_of - mean_row * mean_col
-                )
+                for source in range(2):
+                    part = slice(source * width + j * 128, source * width + (j + 1) * 128)
+                    mean_col = acc_ref[2 * side:2 * side + 1, part] * part_of
+                    pieces.append(acc_ref[place, part] * part_of - mean_row * mean_col)
+            turned = jnp.swapaxes(jnp.stack(pieces, axis=0), 0, 1)
+            out_ref[row_source, first * groups:(first + 8) * groups, :] = turned.reshape(8 * groups, 128)
 
 
 def joint_cov(hidden_out, rows_in, cols_in, call_id):

time: 234 us -> 231 us (0.987)
  Pallas kernels: 230 us -> 226 us
    pallas_call x1, Pallas kernels: 9.42 us -> 5.76 us  [finish(): pl.pallas_call(functools.partial(finish_kernel, all_rows, strips), out_sh...]
where the time goes in v5:
time: 231 us; the launch traced here: 229 us
  Pallas kernels  226 us (98%)
    pallas_call x1, Pallas kernels, front(): pl.pallas_call(functools.partial(front_kernel, chips, kv_heads, groups),...  131 us
    pallas_call x1, Pallas kernels, joint_cov(): pl.pallas_call(functools.partial(cov_kernel, chips), out_shape=[jax.Shape...  89.7 us
    pallas_call x1, Pallas kernels, finish(): pl.pallas_call(functools.partial(finish_kernel, all_rows, strips), out_sh...  5.76 us

profile of v5, /device:TPU:0, one launch (start us, length us, event | category | flops | bytes accessed | tf_op | source)
XLA Modules:
  0.0 229.2 jit_solution(9009189891632532000)
XLA Ops:
  0.7 0.5 fusion
  1.2 0.0 copy-start
  1.2 0.7 copy-done
  1.9 0.0 copy-start.1
  1.9 0.7 copy-done.1
  2.6 131.0 %front.1 = (bf16[256,2048]{1,0:T(8,128)(2,1)S(1)}, bf16[4096,2048]{1,0:T(8,128)(2,1)}, bf16[32768,256]{1,0:T(8,128)(2,1)}) custom-call(bf16[256,2048]{1,0:T(8,128)(2,1)} %x_ref.1, f32[1,4096]{1,0:T(1,128)S(1)} %bitcast.7, f32[256,128]{1,0:T(8,128)S(1)} %get-tuple-element.17.cos_ref, f32[256,128]{1,0:T(8,128)S(1)} %get-tuple-element.16.sin_ref, ...), custom_call_target="tpu_custom_call" | custom-call | tf_op jit(solution)/shard_map/front/pallas_call | solution.py:968
  133.7 89.7 %cov_ring.1 = (f32[528,4096]{1,0:T(8,128)S(1)}, f32[512,128]{1,0:T(8,128)S(1)}) custom-call(bf16[256,2048]{1,0:T(8,128)(2,1)S(1)} %get-tuple-element.9.x_ref, bf16[4096,2048]{1,0:T(8,128)(2,1)} %get-tuple-element.10.cin_ref, bf16[32768,256]{1,0:T(8,128)(2,1)} %get-tuple-element.11.rin_ref), custom_call_target="tpu_custom_call" | custom-call | flops 68719476736 | bytes 46137344 | tf_op jit(solution)/shard_map/cov_ring/pallas_call | solution.py:621
  223.4 5.8 %finish.1 = (f32[2,8192,128]{2,1,0:T(8,128)}, bf16[256,2048]{1,0:T(8,128)(2,1)}) custom-call(f32[528,4096]{1,0:T(8,128)S(1)} %get-tuple-element.12.acc_ref, f32[512,128]{1,0:T(8,128)S(1)} %get-tuple-element.13.rsum_ref, bf16[256,2048]{1,0:T(8,128)(2,1)S(1)} %get-tuple-element.9.x_ref), custom_call_target="tpu_custom_call" | custom-call | tf_op jit(solution)/shard_map/finish/pallas_call | solution.py:662
  (2 shorter events, 0.0 us)
Async XLA Ops:
  1.2 0.7 copy-start
  1.9 0.7 copy-start.1

commit v6 on v5

--- a/solution.py
+++ b/solution.py
@@ -525,7 +525,7 @@
     acc_ref[...] = jnp.zeros_like(acc_ref)
     rsum_ref[...] = jnp.zeros_like(rsum_ref)
     own.wait()
-    tile = min(512, width)
+    tile = min(1024, width)
 
     def work(step, mine):
         if not mine:

time: 231 us -> 230 us (level)
  no operation moved by 1% of the time
where the time goes in v6:
time: 230 us; the launch traced here: 228 us
  Pallas kernels  226 us (98%)
    pallas_call x1, Pallas kernels, front(): pl.pallas_call(functools.partial(front_kernel, chips, kv_heads, groups),...  131 us
    pallas_call x1, Pallas kernels, joint_cov(): pl.pallas_call(functools.partial(cov_kernel, chips), out_shape=[jax.Shape...  89 us
    pallas_call x1, Pallas kernels, finish(): pl.pallas_call(functools.partial(finish_kernel, all_rows, strips), out_sh...  5.76 us

profile of v6, /device:TPU:0, one launch (start us, length us, event | category | flops | bytes accessed | tf_op | source)
XLA Modules:
  0.0 228.5 jit_solution(12258131226424603249)
XLA Ops:
  0.7 0.5 fusion
  1.2 0.0 copy-start
  1.2 0.7 copy-done
  1.9 0.0 copy-start.1
  1.9 0.7 copy-done.1
  2.6 131.0 %front.1 = (bf16[256,2048]{1,0:T(8,128)(2,1)S(1)}, bf16[4096,2048]{1,0:T(8,128)(2,1)}, bf16[32768,256]{1,0:T(8,128)(2,1)}) custom-call(bf16[256,2048]{1,0:T(8,128)(2,1)} %x_ref.1, f32[1,4096]{1,0:T(1,128)S(1)} %bitcast.7, f32[256,128]{1,0:T(8,128)S(1)} %get-tuple-element.17.cos_ref, f32[256,128]{1,0:T(8,128)S(1)} %get-tuple-element.16.sin_ref, ...), custom_call_target="tpu_custom_call" | custom-call | tf_op jit(solution)/shard_map/front/pallas_call | solution.py:968
  133.7 89.0 %cov_ring.1 = (f32[528,4096]{1,0:T(8,128)S(1)}, f32[512,128]{1,0:T(8,128)S(1)}) custom-call(bf16[256,2048]{1,0:T(8,128)(2,1)S(1)} %get-tuple-element.9.x_ref, bf16[4096,2048]{1,0:T(8,128)(2,1)} %get-tuple-element.10.cin_ref, bf16[32768,256]{1,0:T(8,128)(2,1)} %get-tuple-element.11.rin_ref), custom_call_target="tpu_custom_call" | custom-call | flops 68719476736 | bytes 46137344 | tf_op jit(solution)/shard_map/cov_ring/pallas_call | solution.py:621
  222.7 5.8 %finish.1 = (f32[2,8192,128]{2,1,0:T(8,128)}, bf16[256,2048]{1,0:T(8,128)(2,1)}) custom-call(f32[528,4096]{1,0:T(8,128)S(1)} %get-tuple-element.12.acc_ref, f32[512,128]{1,0:T(8,128)S(1)} %get-tuple-element.13.rsum_ref, bf16[256,2048]{1,0:T(8,128)(2,1)S(1)} %get-tuple-element.9.x_ref), custom_call_target="tpu_custom_call" | custom-call | tf_op jit(solution)/shard_map/finish/pallas_call | solution.py:662
  (2 shorter events, 0.0 us)
Async XLA Ops:
  1.2 0.7 copy-start
  1.9 0.7 copy-start.1
